TPU v7x, 128 devices: a whole 4x4x4 slice. The times are simulated.
128 devices in a mesh: row: 8 (over z, core), col: 4 (over y), layer: 4 (over x).
Axes of the slice: x: 4, y: 4, z: 4, core: 2. Of those that a mesh axis runs over, the one named last changes fastest.
Arguments:
- blocks: bfloat16 [512, 24, 128, 128], P(('row', 'col'), 'layer'), may hold values from -2 to 2
- pattern: int32 [512, 24], replicated, may hold values from 0 to 511, as said below
- out_pattern: int32 [512, 24], replicated, may hold values from 0 to 511, as said below
Outputs:
- product: bfloat16 [512, 24, 128, 128], P(('row', 'col'), 'layer')
Inputs may be any that keep to these rules, and one draw needn't show every extreme that they name: `pattern`: block row i stores the block columns (i + d) mod 512 for 24 distinct offsets d from -12 to 12, always including 0, -12 and 12, in no particular order. `out_pattern`: the same law as pattern, drawn independently.
All inputs are finite; a program needn't handle non-finite values.
Results may differ from a plain program's by a relative error of at most 0.001.
Values may be sent and summed in bfloat16 or wider, within the bound.
No kernel may reach another device: no remote copies, remote signals or barrier semaphores. Data moves between devices by JAX's collectives and lax.ppermute only.
A program may use at most 192 MiB of HBM per device.

v0:
```python
import jax
import jax.numpy as jnp
from jax import lax
from jax.sharding import PartitionSpec as P

REACH = 12


def with_halo(cells, sides, width):
    for axis, dim in sides:
        count = lax.axis_size(axis)
        head = lax.slice_in_dim(cells, 0, width, axis=dim)
        tail = lax.slice_in_dim(cells, cells.shape[dim] - width, cells.shape[dim], axis=dim)
        cells = jnp.concatenate(
            [
                lax.ppermute(tail, axis, [(i, (i + 1) % count) for i in range(count)]),
                cells,
                lax.ppermute(head, axis, [((i + 1) % count, i) for i in range(count)]),
            ],
            axis=dim,
        )
    return cells


def row_terms(left, right, right_cols, out_cols):
    match = right_cols[:, :, None] == out_cols[None, None, :]
    found = jnp.any(match, axis=1)
    picked = jnp.argmax(match.astype(jnp.int32), axis=1)
    chosen = jnp.take_along_axis(right, picked[:, :, None, None], axis=1)
    chosen = jnp.where(found[:, :, None, None], chosen, jnp.zeros((), right.dtype))
    return jnp.einsum("tab,tsbc->sac", left, chosen, preferred_element_type=jnp.float32)


def run_rows(left, left_cols, out_cols, outer, pattern, lowest):
    total_rows = pattern.shape[0]

    def one_row(item):
        piece, piece_cols, wanted = item
        where = (piece_cols - lowest) % total_rows
        right = jnp.take(outer, where, axis=0)
        right_cols = jnp.take(pattern, piece_cols, axis=0)
        return row_terms(piece, right, right_cols, wanted)

    return lax.map(one_row, (left, left_cols, out_cols))


def layer_reduce(partial_value):
    return lax.psum_scatter(partial_value, "layer", scatter_dimension=1, tiled=True).astype(
        jnp.bfloat16
    )


def per_device(blocks, pattern, out_pattern):
    rows_dev = blocks.shape[0]
    slot_dev = blocks.shape[1]
    first = lax.axis_index(("row", "col")) * rows_dev
    layer_start = lax.axis_index("layer") * slot_dev
    own_cols = lax.dynamic_slice_in_dim(pattern, first, rows_dev, 0)
    own_out = lax.dynamic_slice_in_dim(out_pattern, first, rows_dev, 0)
    lowest = first - REACH
    whole = lax.all_gather(blocks, "layer", axis=1, tiled=True)
    outer = with_halo(whole, ((("row", "col"), 0),), REACH)
    left_cols = lax.dynamic_slice_in_dim(own_cols, layer_start, slot_dev, 1)
    partial_value = run_rows(blocks, left_cols, own_out, outer, pattern, lowest)
    result = layer_reduce(partial_value)
    return result


def solution(mesh):
    in_specs = (P(("row", "col"), "layer", None, None), P(), P())
    out_specs = P(("row", "col"), "layer", None, None)
    return jax.shard_map(
        per_device, mesh=mesh, in_specs=in_specs, out_specs=out_specs, check_vma=False
    )
```

profile of v0, /device:TPU:57, one launch (start us, length us, event | category | flops | bytes accessed | tf_op | source)
XLA Modules:
  0.0 1470.9 jit_solution(14778424415035127037)
XLA Ops:
  7.3 121.8 %all-gather.2.cloned.1.call-done = bf16[16,24,128,128]{3,2,1,0:T(8,128)(2,1)} async-done(((bf16[16,6,128,128]{3,2,1,0:T(8,128)(2,1)}), bf16[16,24,128,128]{3,2,1,0:T(8,128)(2,1)}) %all-gather.2.cloned.1.call-update) | async-done | bytes 12582928 | tf_op jit(solution)/shard_map/all_gather | solution.py:61
  129.1 14.9 %fusion.21 = (bf16[12,24,128,128]{3,2,1,0:T(8,128)(2,1)}, bf16[12,24,128,128]{3,2,1,0:T(8,128)(2,1)}) fusion(bf16[16,24,128,128]{3,2,1,0:T(8,128)(2,1)} %all-gather.2.cloned.1.call-done), kind=kLoop, calls=%fused_computation.51 | loop fusion | bytes 37748736 | tf_op jit(solution)/shard_map/slice | solution.py:13
  147.6 200.5 %collective-permute-done = bf16[12,24,128,128]{3,2,1,0:T(8,128)(2,1)} collective-permute-done((bf16[12,24,128,128]{3,2,1,0:T(8,128)(2,1)}, bf16[12,24,128,128]{3,2,1,0:T(8,128)(2,1)}, u32[]{:S(2)}, u32[]{:S(2)}) %collective-permute-start) | collective-permute-done | bytes 9437216 | tf_op jit(solution)/shard_map/ppermute | solution.py:16
  351.9 21.8 %pad_maximum_fusion = bf16[40,24,128,128]{3,2,1,0:T(8,128)(2,1)} fusion(bf16[12,24,128,128]{3,2,1,0:T(8,128)(2,1)} %collective-permute-done.1, bf16[16,24,128,128]{3,2,1,0:T(8,128)(2,1)} %all-gather.2.cloned.1.call-done, bf16[12,24,128,128]{3,2,1,0:T(8,128)(2,1)} %collective-permute-done), kind=kLoop, calls=%fused_computation.48 | loop fusion | flops 31457280 | bytes 62914560 | tf_op jit(solution)/shard_map/concatenate | solution.py:14
  373.6 659.9 %while.12 = (s32[]{:T(128)}, f32[16,24,128,128]{3,2,1,0:T(8,128)}, s32[16,6]{1,0:T(8,128)S(1)}, s32[512,24]{1,0:T(8,128)S(1)}, s32[16,24]{1,0:T(8,128)S(1)}, /*i...) while((s32[]{:T(128)}, f32[16,24,128,128]{3,2,1,0:T(8,128)}, ...), condition=%wide.region_3.4_spmd, body=%wide.region_0.3_spmd.sunk | while | flops 611099008 | bytes 41110260 | solution.py:44
  375.1 13.5 gather_fusion
  393.7 14.5 gather_fusion.2
  416.4 13.5 gather_fusion
  435.0 14.5 gather_fusion.2
  457.6 13.5 gather_fusion
  476.2 14.5 gather_fusion.2
  498.9 13.5 gather_fusion
  517.4 14.5 gather_fusion.2
  540.1 13.5 gather_fusion
  558.7 14.5 gather_fusion.2
  581.4 13.5 gather_fusion
  599.9 14.5 gather_fusion.2
  622.6 13.5 gather_fusion
  641.1 14.5 gather_fusion.2
  663.9 13.5 gather_fusion
  682.4 14.5 gather_fusion.2
  723.7 14.5 gather_fusion.2
  764.9 14.5 gather_fusion.2
  787.6 13.5 gather_fusion
  806.1 14.5 gather_fusion.2
  847.4 14.5 gather_fusion.2
  888.6 14.5 gather_fusion.2
  929.8 14.5 gather_fusion.2
  952.5 13.5 gather_fusion
  971.0 14.5 gather_fusion.2
  1012.3 14.5 gather_fusion.2
  1033.5 426.6 %all-reduce.2 = bf16[16,24,128,128]{3,2,1,0:T(8,128)(2,1)} all-reduce(f32[16,24,128,128]{3,2,1,0:T(8,128)} %get-tuple-element.108), channel_id=2, replica_groups=mesh['row'=8,'col'=4,'layer'=4] {'layer'}, use_global_device_ids=true, to_apply=%region_4.5.clone | all-reduce | flops 6291456 | bytes 37748736
  (282 shorter events, 304.0 us)
Async XLA Ops:
  6.5 139.5 %copy-start = (s32[512,24]{0,1:T(8,128)S(1)}, s32[512,24]{0,1:T(8,128)}, u32[]{:S(2)}) copy-start(s32[512,24]{0,1:T(8,128)} %param.7) | copy-start | bytes 147460
  6.5 122.6 %all-gather.2.cloned.1.call-start = ((), (), s32[]{:S(2)}) async-start(), calls=%async_computation | async-start | bytes 15728640 | tf_op jit(solution)/shard_map/all_gather | solution.py:61
  7.3 138.7 %copy-start.2 = (s32[512,24]{0,1:T(8,128)S(1)}, s32[512,24]{0,1:T(8,128)}, u32[]{:S(2)}) copy-start(s32[512,24]{0,1:T(8,128)} %param.6) | copy-start | bytes 147460
  7.3 139.0 %copy-start.3 = (u32[128]{0:T(128)S(1)}, u32[128]{0:T(128)}, u32[]{:S(2)}) copy-start(u32[128]{0:T(128)} %constant.179) | copy-start | bytes 1540
  144.0 204.1 %collective-permute-start = (bf16[12,24,128,128]{3,2,1,0:T(8,128)(2,1)}, bf16[12,24,128,128]{3,2,1,0:T(8,128)(2,1)}, u32[]{:S(2)}, u32[]{:S(2)}) collective-permute-start(bf16[12,24,128,128]{3,2,1,0:T(8,128)(2,1)} %get-tuple-element.163), channel_id=1, source_target_pairs={{0,4},{4,8},{8,12},{12,16},{16,20},{20,24},{24,28},{28,32},{32,36}... | collective-permute-start | bytes 28311560 | tf_op jit(solution)/shard_map/ppermute | solution.py:16
  145.9 206.0 %collective-permute-start.1 = (bf16[12,24,128,128]{3,2,1,0:T(8,128)(2,1)}, bf16[12,24,128,128]{3,2,1,0:T(8,128)(2,1)}, u32[]{:S(2)}, u32[]{:S(2)}) collective-permute-start(bf16[12,24,128,128]{3,2,1,0:T(8,128)(2,1)} %get-tuple-element.164), channel_id=1, source_target_pairs={{4,0},{8,4},{12,8},{16,12},{20,16},{24,20},{28,24},{32,28},{36,32}... | collective-permute-start | bytes 28311560 | tf_op jit(solution)/shard_map/ppermute | solution.py:18
  1033.5 430.6 %copy-start.1 = (s32[512,24]{0,1:T(8,128)S(1)}, s32[512,24]{0,1:T(8,128)}, u32[]{:S(2)}) copy-start(s32[512,24]{0,1:T(8,128)} %param.7) | copy-start | bytes 147460
Sparse Core Ops, SparseCore 0:
  9.0 120.0 all-gather.1
where the time goes:
time: 1470 us
  local copies, waits for them, and re-layouts  505 us (34%)
  blocking collectives  427 us (29%)
  waiting for transfers between devices  327 us (22%)
  other arithmetic  118 us (8%)
  matrix products  77.7 us (5%)
    unnamed x1, blocking collectives  427 us
    gather x32, local copies, waits for them, and re-layouts, row_terms(): chosen = jnp.take_along_axis(right, picked[:, :, None, None], axis=1)  233 us
    gather x16, local copies, waits for them, and re-layouts, one_row(): right = jnp.take(outer, where, axis=0)  215 us
    ppermute x1, waiting for transfers between devices, with_halo(): lax.ppermute(tail, axis, [(i, (i + 1) % count) for i in range(count)])  201 us
    all_gather x1, waiting for transfers between devices, per_device(): whole = lax.all_gather(blocks, 'layer', axis=1, tiled=True)  122 us
    select_n x16, other arithmetic, one_row(): right = jnp.take(outer, where, axis=0)  81.1 us
    dot_general x16, matrix products, row_terms(): jnp.einsum('tab,tsbc->sac', left, chosen, preferred_element_type=jnp.floa...  77.7 us
  transfers between devices with their start and end apart: 3, of which 3 were waited for; matrix products, arithmetic and copies ran while one was open for 0% of the time, Pallas kernels for 0%

commit v1 on v0

v1 whole, which is shorter than its diff:
```python
import jax
import jax.numpy as jnp
import numpy as np
from jax import lax
from jax.experimental import pallas as pl
from jax.experimental.pallas import tpu as pltpu
from jax.sharding import PartitionSpec as P


AXES = ("row", "col", "layer")
B = 128
SLOTS = 24
TOTAL = 512
WIN = 28
BF = jnp.bfloat16
F32 = jnp.float32

RIGHT = 0
LEFT = RIGHT + 32 * WIN
KEPT = LEFT + 4 * 32
PLACE = KEPT + 4 * SLOTS
HOME = PLACE + 1
ZERO = 576
NEAR = 96


def dev(z, c, y, x):
    return ((2 * z + c) * 4 + y) * 4 + x


def devices():
    return [(z, c, y, x) for z in range(4) for c in range(2) for y in range(4) for x in range(4)]


def is_home(c, x):
    return c == (1 if x >= 2 else 0)


def is_first(x):
    return x in (0, 3)


def after(z, c, y, x):
    if y < 3:
        return (z, c, y + 1, x)
    if x < 2:
        return (z, c, 0, 3 - x)
    return ((z + 1) % 4, c, 0, 3 - x)


def before(z, c, y, x):
    if y > 0:
        return (z, c, y - 1, x)
    if x >= 2:
        return (z, c, 3, 3 - x)
    return ((z - 1) % 4, c, 3, 3 - x)


PAIRS_SHARE = [
    (dev(z, c, y, x), dev(z, c, y, x ^ 1) if is_home(c, x) else dev(z, 1 - c, y, 3 - x))
    for z, c, y, x in devices()
]
PAIRS_PASS = [(dev(z, c, y, x), dev(z, c, y, x ^ 1)) for z, c, y, x in devices() if not is_home(c, x)]
PAIRS_UP = [(dev(*d), dev(*after(*d))) for d in devices()]
PAIRS_DOWN = [(dev(*d), dev(*before(*d))) for d in devices()]
PAIRS_WIDE = [(dev(*d), dev(*(after(*d) if is_first(d[3]) else before(*d)))) for d in devices()]
PAIRS_NARROW = [(dev(*d), dev(*(before(*d) if is_first(d[3]) else after(*d)))) for d in devices()]
PAIRS_RELAY = [(dev(z, c, y, x), dev(z, c, y, x ^ 1)) for z, c, y, x in devices()]
PAIRS_SWAP = [(dev(z, c, y, x), dev(z, 1 - c, y, x)) for z, c, y, x in devices()]
AT_HOME = {dev(z, c, y, x) for z, c, y, x in devices() if is_home(c, x)}


def from_home(pairs):
    return [p for p in pairs if p[0] in AT_HOME]


def from_guest(pairs):
    return [p for p in pairs if p[0] not in AT_HOME]


def pairs_out(k, places):
    pairs = []
    for z in range(4):
        for y in range(4):
            for t in range(2):
                for n in places:
                    chip = ((0, 1), (3, 2))[t][n // 2]
                    pairs.append((dev(z, n % 2, y, chip), dev(z, t, y, n ^ k)))
    return pairs


def send(value, pairs):
    return lax.ppermute(value, AXES, pairs)


class Loads:
    def __init__(self, dest, sems):
        self.dest, self.sems, self.waits = dest, sems, []

    def add(self, choices, at, size):
        q = len(self.waits)
        for flag, src, first in choices:

            def go(src=src, first=first):
                pltpu.make_async_copy(
                    src.at[pl.ds(first, size)], self.dest.at[pl.ds(at, size)], self.sems.at[q]
                ).start()

            if flag is None:
                go()
            else:
                pl.when(flag)(go)
        src, first = choices[0][1:]
        self.waits.append(
            pltpu.make_async_copy(
                src.at[pl.ds(first, size)], self.dest.at[pl.ds(at, size)], self.sems.at[q]
            )
        )

    def wait(self):
        for w in self.waits:
            w.wait()


def products(tab, left, raw, first, depth, put):
    lhs = left[:, : depth * B]

    def pair(p, carry):
        rows = []
        for j in range(depth):
            at = RIGHT + (first + j) * WIN + 2 * p
            rows.append(jnp.concatenate([raw[tab[at]], raw[tab[at + 1]]], axis=1))
        r = jnp.dot(lhs, jnp.concatenate(rows, axis=0), preferred_element_type=F32)
        put(2 * p, r[:, :B])
        put(2 * p + 1, r[:, B:])
        return carry

    lax.fori_loop(0, WIN // 2, pair, 0)


def first_kernel(tab, *refs):
    own, ra, rb, za, zb = (refs[2 * q : 2 * q + 2] for q in range(5))
    halos = (refs[10:16], refs[16:22])
    acc, near, far, raw, left, sems = refs[22:]
    loads = Loads(raw, sems)
    home = tab[HOME] == 1
    away = tab[HOME] == 0
    for side in range(2):
        loads.add([(None, ra[side], 0)], side * 96, 48)
        loads.add([(None, rb[side], 0)], side * 96 + 48, 48)
        here, there = (home, away) if side == 0 else (away, home)
        at = (2 + side) * 96
        loads.add([(here, own[side], 0), (there, za[side], 0)], at, 24)
        loads.add([(here, own[side], 72), (there, za[side], 24)], at + 24, 24)
        loads.add([(here, own[side], 24), (there, zb[side], 0)], at + 48, 48)
    for h, halo in enumerate(halos):
        home, away = tab[HOME + 1 + h] == 1, tab[HOME + 1 + h] == 0
        for side in range(2):
            at = 384 + h * 96
            loads.add([(None, halo[2 + side], 0)], at + side * 24, 24)
            here, there = (home, away) if side == 0 else (away, home)
            loads.add(
                [(here, halo[side], 0), (there, halo[4 + side], 0)], at + (2 + side) * 24, 24
            )
    raw[ZERO] = jnp.zeros((B, B), BF)
    loads.wait()

    def one_row(i, carry):
        rows = pl.ds(pl.multiple_of(i * B, B), B)
        for j in range(32):
            block = raw[tab[LEFT + i * 32 + j]]
            if j < 24:
                left[rows, j * B : (j + 1) * B] = block
            else:
                to = near if j < 28 else far
                to[rows, (j % 4) * B : (j % 4 + 1) * B] = block
        return carry

    lax.fori_loop(0, 4, one_row, 0)

    def put(c, value):
        acc[c] = value

    products(tab, left, raw, 0, 24, put)


def select(tab, total, outs):
    place = tab[PLACE]
    for k in range(4):
        lam = (place ^ k) * 6
        out = outs[k]

        def one_row(i, carry):
            for s in range(6):
                c = tab[KEPT + i * SLOTS + lam + s]
                out[i * 6 + s] = total[c, pl.ds(pl.multiple_of(i * B, B), B)].astype(BF)
            return carry

        lax.fori_loop(0, 4, one_row, 0)


def second_kernel(tab, *refs):
    own, r, z = refs[0:2], refs[2:4], refs[4:6]
    left, acc = refs[6:8]
    outs, total, raw, sems = refs[8:12], refs[12], refs[13], refs[14]
    loads = Loads(raw, sems)
    home, away = tab[HOME + 3] == 1, tab[HOME + 3] == 0
    for side in range(2):
        loads.add([(None, r[side], 0)], side * 24, 24)
        here, there = (home, away) if side == 0 else (away, home)
        loads.add([(here, own[side], 0), (there, z[side], 0)], (2 + side) * 24, 24)
    raw[NEAR] = jnp.zeros((B, B), BF)
    loads.wait()

    def put(c, value):
        total[c] = acc[c] + value

    products(tab, left, raw, 24, 4, put)
    select(tab, total, outs)


def third_kernel(tab, *refs):
    left, acc = refs[4:6]
    outs, raw, total, sems = refs[6:10], refs[10], refs[11], refs[12]
    loads = Loads(raw, sems)
    for q in range(4):
        loads.add([(None, refs[q], 0)], q * 24, 24)
    raw[NEAR] = jnp.zeros((B, B), BF)
    loads.wait()

    def put(c, value):
        total[c] = acc[c] + value

    products(tab, left, raw, 28, 4, put)
    select(tab, total, outs)


def place_kernel(where, *refs):
    early, late, out, sems = refs[:4], refs[4:8], refs[8], refs[9]
    x = where[0]
    for n in range(4):
        for k in range(4):
            src = (early if n in (1, 2) else late)[k]

            @pl.when((x ^ n) == k)
            def _():
                pltpu.make_async_copy(src, out.at[pl.ds(24 * n, 24)], sems.at[n]).start()

    for n in range(4):
        pltpu.make_async_copy(early[0], out.at[pl.ds(24 * n, 24)], sems.at[n]).wait()


ANY = pl.BlockSpec(memory_space=pl.ANY)
VM = pl.BlockSpec(memory_space=pltpu.VMEM)
ACC = jax.ShapeDtypeStruct((WIN, 4 * B, B), F32)
SIDE = jax.ShapeDtypeStruct((4 * B, 4 * B), BF)
OUT = jax.ShapeDtypeStruct((24, B, B), BF)


def call(body, tab, far, near, outs, scratch, vmem, flops, moved):
    single = not isinstance(outs, list)
    return pl.pallas_call(
        body,
        out_shape=outs,
        grid_spec=pltpu.PrefetchScalarGridSpec(
            num_scalar_prefetch=1,
            grid=(),
            in_specs=[ANY] * len(far) + [VM] * len(near),
            out_specs=VM if single else [VM] * len(outs),
            scratch_shapes=scratch,
        ),
        compiler_params=pltpu.CompilerParams(vmem_limit_bytes=vmem * 2**20),
        cost_estimate=pl.CostEstimate(flops=flops, transcendentals=0, bytes_accessed=moved),
    )(tab, *far, *near)


def sems(n):
    return pltpu.SemaphoreType.DMA((n,))


def tables(pattern, out_pattern):
    row = lax.axis_index("row")
    y = lax.axis_index("col")
    x = lax.axis_index("layer")
    c = row % 2
    first = jnp.logical_or(x == 0, x == 3)
    group = ((row // 2) * 2 + (x >= 2).astype(jnp.int32)) * 4 + y
    place = jnp.where(first, 0, 2) + c
    top = 16 * group
    base = top + 4 * place - 12
    near = np.arange(4)
    fixed = np.concatenate([near, near + 12, np.arange(4, 12), near - 4, near + 16])
    sec = jnp.where(first, near - 8, near + 20)
    third = jnp.where(first, near - 12, near + 24)
    rows = (top + jnp.concatenate([jnp.asarray(fixed, jnp.int32), sec, third])) % TOTAL
    found = jnp.take(pattern, rows, axis=0)

    def is_home_of(chip, core):
        return (core == (chip >= 2).astype(jnp.int32)).astype(jnp.int32)

    def held(chip):
        out = []
        for core in (c, 1 - c):
            home = is_home_of(chip, core) == 1
            out.append((jnp.where(home, chip ^ 1, 3 - chip), jnp.where(home, chip, (3 - chip) ^ 1)))
        return [out[0][0], out[1][0], out[0][1], out[1][1]]

    low = jnp.where(y == 0, 3 - x, x)
    high = jnp.where(y == 3, 3 - x, x)
    wide = jnp.where(first, low, high)
    direct, relay = held(wide), held(wide ^ 1)
    lam = jnp.stack(
        [jnp.stack(v) for v in (held(x), held(low), held(high), held(wide), direct[:2] + relay[:2])]
    )
    kind = jnp.sum(
        jnp.where(lam[:, None, :] == jnp.arange(4)[None, :, None], jnp.arange(4), 0), axis=-1
    )
    packs = np.array([16, 4, 4, 4, 4])
    pack = np.repeat(np.arange(5), packs)
    kinds = jnp.repeat(kind, packs, axis=0, total_repeat_length=32)
    start = np.array([0, 384, 480, 0, 0])[pack] + 6 * np.concatenate([np.arange(n) for n in packs])
    per_kind = np.array([96, 24, 24, 24, 24])[pack]
    pos = start[:, None, None] + per_kind[:, None, None] * kinds[:, :, None] + np.arange(6)
    pos = pos.reshape(32, SLOTS)
    empty = np.where(np.arange(32) < 24, ZERO, NEAR)[:, None]
    rel = (found - base) % TOTAL
    hit = rel[:, :, None] == jnp.arange(WIN)
    right = jnp.sum(jnp.where(hit, pos[:, :, None] - empty[:, :, None], 0), axis=1) + empty
    at = jnp.where(place == 0, 0, jnp.where(place == 3, 4, jnp.where(place == 1, 8, 12)))
    mine = lax.dynamic_slice_in_dim(found, at, 4, 0)
    spot = lax.dynamic_slice_in_dim(pos, at, 4, 0)
    hit = mine[:, :, None] == rows
    left = jnp.sum(jnp.where(hit, spot[:, :, None] - ZERO, 0), axis=1) + ZERO
    unit = (top + 4 * place + jnp.arange(4)) % TOTAL
    kept = (jnp.take(out_pattern, unit, axis=0) - base) % TOTAL
    small = jnp.stack(
        [place, is_home_of(x, c), is_home_of(low, c), is_home_of(high, c), is_home_of(wide, c)]
    )
    return jnp.concatenate(
        [right.reshape(-1), left.reshape(-1), kept.reshape(-1), small]
    ).astype(jnp.int32)


def square(blocks, pattern, out_pattern):
    x = lax.axis_index("layer")
    first = jnp.logical_or(x == 0, x == 3)
    tab = tables(pattern, out_pattern)
    own = blocks.reshape(96, B, B)
    unit = jnp.where(first, 24, 0)

    def swap(a, b=PAIRS_SWAP):
        return send(a, b)

    ra = send(jnp.concatenate([own[:24], own[72:]], axis=0), PAIRS_SHARE)
    own_up = send(own[72:], from_home(PAIRS_UP))
    own_down = send(own[:24], from_home(PAIRS_DOWN))
    rb = send(own[24:72], PAIRS_SHARE)
    own_sec = send(lax.dynamic_slice_in_dim(own, 24 + unit, 24, 0), from_home(PAIRS_WIDE))
    own_s = swap(own, from_home(PAIRS_SWAP))

    za = send(ra, PAIRS_PASS)
    r_up, r_down = send(ra[24:], PAIRS_UP), send(ra[:24], PAIRS_DOWN)
    zb = send(rb, PAIRS_PASS)
    rb_unit = lax.dynamic_slice_in_dim(rb, unit, 24, 0)
    rb_other = lax.dynamic_slice_in_dim(rb, 24 - unit, 24, 0)
    r_sec = send(rb_unit, PAIRS_WIDE)
    r_narrow = send(rb_unit, PAIRS_NARROW)
    r_direct = send(rb_other, PAIRS_WIDE)
    z_up, z_down = send(za[24:], from_guest(PAIRS_UP)), send(za[:24], from_guest(PAIRS_DOWN))
    z_sec = send(lax.dynamic_slice_in_dim(zb, unit, 24, 0), from_guest(PAIRS_WIDE))
    r_relay = send(r_narrow, PAIRS_RELAY)

    group = [
        own, own_s,
        ra, swap(ra), rb, swap(rb),
        za, swap(za, from_guest(PAIRS_SWAP)), zb, swap(zb, from_guest(PAIRS_SWAP)),
    ]
    group += [own_up, swap(own_up), r_up, swap(r_up), z_up, swap(z_up)]
    group += [own_down, swap(own_down), r_down, swap(r_down), z_down, swap(z_down)]
    acc, near, far = call(
        first_kernel, tab, group, [], [ACC, SIDE, SIDE],
        [pltpu.VMEM((577, B, B), BF), pltpu.VMEM((4 * B, 24 * B), BF), sems(18)],
        40, 11 * 10**9, 28 * 10**6,
    )
    more = [own_sec, swap(own_sec), r_sec, swap(r_sec), z_sec, swap(z_sec)]
    *ready, acc = call(
        second_kernel, tab, more, [near, acc], [OUT] * 4 + [ACC],
        [pltpu.VMEM((97, B, B), BF), sems(4)],
        26, 2 * 10**9, 20 * 10**6,
    )
    early = [send(r, pairs_out(k, (1, 2))) for k, r in enumerate(ready)]
    more = [r_direct, swap(r_direct), r_relay, swap(r_relay)]
    ready = call(
        third_kernel, tab, more, [far, acc], [OUT] * 4,
        [pltpu.VMEM((97, B, B), BF), pltpu.VMEM((WIN, 4 * B, B), F32), sems(4)],
        26, 2 * 10**9, 14 * 10**6,
    )
    late = [send(r, pairs_out(k, (0, 3))) for k, r in enumerate(ready)]
    out = call(
        place_kernel, x.reshape(1).astype(jnp.int32), early + late, [],
        jax.ShapeDtypeStruct((96, B, B), BF), [sems(4)], 8, 0, 6 * 10**6,
    )
    return out.reshape(16, 6, B, B)


def solution(mesh):
    in_specs = (P(("row", "col"), "layer", None, None), P(), P())
    out_specs = P(("row", "col"), "layer", None, None)
    return jax.shard_map(square, mesh=mesh, in_specs=in_specs, out_specs=out_specs, check_vma=False)
```

time: 1470 us -> 258 us (0.18)
  the two profiles are of different devices: /device:TPU:57 before, /device:TPU:1 now
where the time goes in v1:
time: 258 us
  waiting for transfers between devices  103 us (40%)
  starting transfers between devices  86.9 us (34%)
  Pallas kernels  37.4 us (14%)
  local copies, waits for them, and re-layouts  25.8 us (10%)
  other arithmetic  3.61 us (1%)
    ppermute x40, waiting for transfers between devices, send(): return lax.ppermute(value, AXES, pairs)  103 us
    ppermute x40, starting transfers between devices, send(): return lax.ppermute(value, AXES, pairs)  86.9 us
    pallas_call x4, Pallas kernels, call(): pl.pallas_call(body, out_shape=outs, grid_spec=pltpu.PrefetchScalarGridSp...  37.4 us
    unnamed x50, local copies, waits for them, and re-layouts  8.62 us
  transfers between devices with their start and end apart: 40, of which 13 were waited for; matrix products, arithmetic and copies ran while one was open for 6% of the time, Pallas kernels for 12%

profile of v1, /device:TPU:1, one launch (start us, length us, event | category | flops | bytes accessed | tf_op | source)
XLA Modules:
  0.0 257.6 jit_solution(6610057279965593313)
XLA Ops:
  0.0 2.7 %fusion.10 = (bf16[4,6,128,128]{3,2,1,0:T(8,128)(2,1)}, bf16[4,6,128,128]{3,2,1,0:T(8,128)(2,1)}) fusion(bf16[16,6,128,128]{3,2,1,0:T(8,128)(2,1)} %param.16), kind=kLoop, calls=%fused_computation.69 | loop fusion | bytes 3145728 | tf_op jit(solution)/shard_map/slice | solution.py:354
  2.7 2.7 %pad_maximum_fusion = bf16[48,128,128]{2,1,0:T(8,128)(2,1)} fusion(bf16[24,128,128]{2,1,0:T(8,128)(2,1)} %bitcast.36, bf16[24,128,128]{2,1,0:T(8,128)(2,1)} %bitcast.35), kind=kLoop, calls=%fused_computation.3 | loop fusion | flops 786432 | bytes 3145728 | tf_op jit(solution)/shard_map/concatenate | solution.py:354
  5.4 3.9 %collective-permute-start.9 = (bf16[48,128,128]{2,1,0:T(8,128)(2,1)}, bf16[48,128,128]{2,1,0:T(8,128)(2,1)S(1)}, u32[]{:S(2)}, u32[]{:S(2)}) collective-permute-start(bf16[48,128,128]{2,1,0:T(8,128)(2,1)} %pad_maximum_fusion), channel_id=1, source_target_pairs={{0,1},{1,0},{2,17},{3,16},{4,5},{5,4},{6,21},{7,20},{8,9},{9,8},{1... | collective-permute-start | bytes 4718600 | tf_op jit(solution)/shard_map/ppermute | solution.py:93
  9.2 2.7 %slice.52 = bf16[8,6,128,128]{3,2,1,0:T(8,128)(2,1)} slice(bf16[16,6,128,128]{3,2,1,0:T(8,128)(2,1)} %param.16), slice={[4:12], [0:6], [0:128], [0:128]} | slice | bytes 3145728 | tf_op jit(solution)/shard_map/slice | solution.py:357
  16.5 22.3 %collective-permute-done.15.refs_10_ = bf16[24,128,128]{2,1,0:T(8,128)(2,1)S(1)} collective-permute-done((bf16[24,128,128]{2,1,0:T(8,128)(2,1)}, bf16[24,128,128]{2,1,0:T(8,128)(2,1)S(1)}, u32[]{:S(2)}, u32[]{:S(2)}) %collective-permute-start.15) | collective-permute-done | bytes 786464 | tf_op jit(solution)/shard_map/ppermute | solution.py:93
  38.8 3.3 %collective-permute-start.22 = (bf16[24,128,128]{2,1,0:T(8,128)(2,1)S(1)}, bf16[24,128,128]{2,1,0:T(8,128)(2,1)}, u32[]{:S(2)}, u32[]{:S(2)}) collective-permute-start(bf16[24,128,128]{2,1,0:T(8,128)(2,1)S(1)} %collective-permute-done.21.refs_16_), channel_id=1, source_target_pairs={{0,16},{1,17},{2,18},{3,19},{4,20},{5,21},{6,22},{7,23},{8,24},{9,... | collective-permute-start | bytes 2359304 | tf_op jit(solution)/shard_map/ppermute | solution.py:93
  43.5 12.1 %collective-permute-done.refs_0_ = bf16[24,128,128]{2,1,0:T(8,128)(2,1)S(1)} collective-permute-done((bf16[24,128,128]{2,1,0:T(8,128)(2,1)S(1)}, bf16[24,128,128]{2,1,0:T(8,128)(2,1)S(1)}, u32[]{:S(2)}, u32[]{:S(2)}) %collective-permute-start) | collective-permute-done | bytes 786464 | tf_op jit(solution)/shard_map/ppermute | solution.py:93
  57.5 9.2 %collective-permute-start.12 = (bf16[48,128,128]{2,1,0:T(8,128)(2,1)S(1)}, bf16[48,128,128]{2,1,0:T(8,128)(2,1)}, u32[]{:S(2)}, u32[]{:S(2)}) collective-permute-start(bf16[48,128,128]{2,1,0:T(8,128)(2,1)S(1)} %collective-permute-done.9.refs_2_), channel_id=1, source_target_pairs={{2,3},{3,2},{6,7},{7,6},{10,11},{11,10},{14,15},{15,14},{16,17},{1... | collective-permute-start | bytes 4718600 | tf_op jit(solution)/shard_map/ppermute | solution.py:93
  69.0 2.7 %constant_dynamic-slice_fusion.4 = (bf16[24,128,128]{2,1,0:T(8,128)(2,1)}, bf16[24,128,128]{2,1,0:T(8,128)(2,1)}) fusion(bf16[48,128,128]{2,1,0:T(8,128)(2,1)} %collective-permute-done.2.refs_4_, s32[]{:T(128)S(6)} %select_n.312, s32[]{:T(128)S(6)} %select_n.310), kind=kLoop, calls=%fused_computation.48 | loop fusion | bytes 3145736 | tf_op jit(solution)/shard_map/dynamic_slice | solution.py:365
  72.6 15.7 %collective-permute-start.33 = (bf16[24,128,128]{2,1,0:T(8,128)(2,1)}, bf16[24,128,128]{2,1,0:T(8,128)(2,1)}, u32[]{:S(2)}, u32[]{:S(2)}) collective-permute-start(bf16[24,128,128]{2,1,0:T(8,128)(2,1)} %get-tuple-element.50), channel_id=1, source_target_pairs={{0,111},{1,5},{2,6},{3,12},{4,0},{5,9},{6,10},{7,3},{8,4},{9,13},{... | collective-permute-start | bytes 2359304 | tf_op jit(solution)/shard_map/ppermute | solution.py:93
  88.4 18.0 %collective-permute-done.3.refs_2_ = bf16[24,128,128]{2,1,0:T(8,128)(2,1)S(1)} collective-permute-done((bf16[24,128,128]{2,1,0:T(8,128)(2,1)}, bf16[24,128,128]{2,1,0:T(8,128)(2,1)S(1)}, u32[]{:S(2)}, u32[]{:S(2)}) %collective-permute-start.3) | collective-permute-done | bytes 786464 | tf_op jit(solution)/shard_map/ppermute | solution.py:93
  106.5 6.9 %collective-permute-start.5 = (bf16[48,128,128]{2,1,0:T(8,128)(2,1)}, bf16[48,128,128]{2,1,0:T(8,128)(2,1)}, u32[]{:S(2)}, u32[]{:S(2)}) collective-permute-start(bf16[48,128,128]{2,1,0:T(8,128)(2,1)} %collective-permute-done.2.refs_4_), channel_id=1, source_target_pairs={{2,3},{3,2},{6,7},{7,6},{10,11},{11,10},{14,15},{15,14},{16,17},{1... | collective-permute-start | bytes 4718600 | tf_op jit(solution)/shard_map/ppermute | solution.py:93
  113.4 7.5 %collective-permute-done.31.refs_0_ = bf16[24,128,128]{2,1,0:T(8,128)(2,1)S(1)} collective-permute-done((bf16[24,128,128]{2,1,0:T(8,128)(2,1)}, bf16[24,128,128]{2,1,0:T(8,128)(2,1)S(1)}, u32[]{:S(2)}, u32[]{:S(2)}) %collective-permute-start.31) | collective-permute-done | bytes 786464 | tf_op jit(solution)/shard_map/ppermute | solution.py:93
  127.9 2.2 collective-permute-start.19
  130.1 2.9 %collective-permute-done.5.refs_8_ = bf16[48,128,128]{2,1,0:T(8,128)(2,1)} collective-permute-done((bf16[48,128,128]{2,1,0:T(8,128)(2,1)}, bf16[48,128,128]{2,1,0:T(8,128)(2,1)}, u32[]{:S(2)}, u32[]{:S(2)}) %collective-permute-start.5) | collective-permute-done | bytes 1572896 | tf_op jit(solution)/shard_map/ppermute | solution.py:93
  133.0 5.0 %collective-permute-start.25 = (bf16[24,128,128]{2,1,0:T(8,128)(2,1)S(1)}, bf16[24,128,128]{2,1,0:T(8,128)(2,1)}, u32[]{:S(2)}, u32[]{:S(2)}) collective-permute-start(bf16[24,128,128]{2,1,0:T(8,128)(2,1)S(1)} %get-tuple-element.51), channel_id=1, source_target_pairs={{2,13},{3,12},{6,2},{7,3},{10,6},{11,7},{14,10},{15,11},{16,127},{... | collective-permute-start | bytes 2359304 | tf_op jit(solution)/shard_map/ppermute | solution.py:93
  138.1 2.4 collective-permute-start.13
  140.5 2.5 collective-permute-start.14
  143.2 2.1 constant_dynamic-slice_fusion.3
  145.3 2.9 %collective-permute-done.34.refs_2_ = bf16[24,128,128]{2,1,0:T(8,128)(2,1)S(1)} collective-permute-done((bf16[24,128,128]{2,1,0:T(8,128)(2,1)}, bf16[24,128,128]{2,1,0:T(8,128)(2,1)S(1)}, u32[]{:S(2)}, u32[]{:S(2)}) %collective-permute-start.34) | collective-permute-done | bytes 786464 | tf_op jit(solution)/shard_map/ppermute | solution.py:93
  148.2 2.2 collective-permute-start.6
  152.2 6.5 %collective-permute-done.6.refs_4_ = bf16[24,128,128]{2,1,0:T(8,128)(2,1)} collective-permute-done((bf16[24,128,128]{2,1,0:T(8,128)(2,1)}, bf16[24,128,128]{2,1,0:T(8,128)(2,1)}, u32[]{:S(2)}, u32[]{:S(2)}) %collective-permute-start.6) | collective-permute-done | bytes 786464 | tf_op jit(solution)/shard_map/ppermute | solution.py:93
  158.7 8.5 %collective-permute-start.1 = (bf16[24,128,128]{2,1,0:T(8,128)(2,1)}, bf16[24,128,128]{2,1,0:T(8,128)(2,1)S(1)}, u32[]{:S(2)}, u32[]{:S(2)}) collective-permute-start(bf16[24,128,128]{2,1,0:T(8,128)(2,1)} %copy-done.1), channel_id=1, source_target_pairs={{0,16},{1,17},{2,18},{3,19},{4,20},{5,21},{6,22},{7,23},{8,24},{9,... | collective-permute-start | bytes 2359304 | tf_op jit(solution)/shard_map/ppermute | solution.py:93
  171.7 24.3 %shard_map.136 = (f32[28,512,128]{2,1,0:T(8,128)}, bf16[512,512]{1,0:T(8,128)(2,1)S(1)}, bf16[512,512]{1,0:T(8,128)(2,1)S(1)}) custom-call(s32[1125]{0:T(1024)S(1)} %concatenate.42.tab, bf16[96,128,128]{2,1,0:T(8,128)(2,1)} %bitcast.33.refs_0_, bf16[96,128,128]{2,1,0:T(8,128)(2,1)} %collective-permute-done.8.refs_1_, ...), custom_call_target="tpu_custom_call" | custom-call | flops 11000000512 | bytes 28000000 | tf_op jit(solution)/shard_map/pallas_call | solution.py:262
  196.0 3.1 %copy-done = f32[28,512,128]{2,1,0:T(8,128)S(1)} copy-done((f32[28,512,128]{2,1,0:T(8,128)S(1)}, f32[28,512,128]{2,1,0:T(8,128)}, u32[]{:S(2)}) %copy-start) | copy-done | bytes 7340056
  199.1 5.6 %shard_map.137 = (bf16[24,128,128]{2,1,0:T(8,128)(2,1)S(1)}, bf16[24,128,128]{2,1,0:T(8,128)(2,1)S(1)}, bf16[24,128,128]{2,1,0:T(8,128)(2,1)S(1)}, bf16[24,128,128]{2,1,0:T(8,128)(2,1)S(1)}, f32[28,512,128]{2,1,0:T(8,128)S(1)}) custom-call(s32[1125]{0:T(1024)S(1)} %concatenate.42.tab, bf16[24,128,128]{2,1,0:T(8,128)(2,1)S(1)} %copy-done.2, ...), custom_call_target="tpu_custom_call" | custom-call | flops 2000000000 | bytes 20000000 | tf_op jit(solution)/shard_map/pallas_call | solution.py:262
  204.7 5.6 %shard_map.138 = (bf16[24,128,128]{2,1,0:T(8,128)(2,1)S(1)}, bf16[24,128,128]{2,1,0:T(8,128)(2,1)S(1)}, bf16[24,128,128]{2,1,0:T(8,128)(2,1)S(1)}, bf16[24,128,128]{2,1,0:T(8,128)(2,1)S(1)}) custom-call(s32[1125]{0:T(1024)S(1)} %concatenate.42.tab, bf16[24,128,128]{2,1,0:T(8,128)(2,1)S(1)} %collective-permute-done.31.refs_0_, ...), custom_call_target="tpu_custom_call" | custom-call | flops 2000000000 | bytes 14000000 | tf_op jit(solution)/shard_map/pallas_call | solution.py:262
  215.7 17.6 %collective-permute-done.36.refs_4_ = bf16[24,128,128]{2,1,0:T(8,128)(2,1)S(1)} collective-permute-done((bf16[24,128,128]{2,1,0:T(8,128)(2,1)S(1)}, bf16[24,128,128]{2,1,0:T(8,128)(2,1)S(1)}, u32[]{:S(2)}, u32[]{:S(2)}) %collective-permute-start.36) | collective-permute-done | bytes 786464 | tf_op jit(solution)/shard_map/ppermute | solution.py:93
  235.2 1.9 collective-permute-start.29
  237.1 8.1 %collective-permute-start.30 = (bf16[24,128,128]{2,1,0:T(8,128)(2,1)S(1)}, bf16[24,128,128]{2,1,0:T(8,128)(2,1)S(1)}, u32[]{:S(2)}, u32[]{:S(2)}) collective-permute-start(bf16[24,128,128]{2,1,0:T(8,128)(2,1)S(1)} %get-tuple-element.34), channel_id=1, source_target_pairs={{16,2},{1,1},{19,18},{2,17},{20,6},{5,5},{23,22},{6,21},{24,10},{9... | collective-permute-start | bytes 2359304 | tf_op jit(solution)/shard_map/ppermute | solution.py:93
  245.2 10.4 %collective-permute-done.28.refs_1_ = bf16[24,128,128]{2,1,0:T(8,128)(2,1)S(1)} collective-permute-done((bf16[24,128,128]{2,1,0:T(8,128)(2,1)S(1)}, bf16[24,128,128]{2,1,0:T(8,128)(2,1)S(1)}, u32[]{:S(2)}, u32[]{:S(2)}) %collective-permute-start.28) | collective-permute-done | bytes 786464 | tf_op jit(solution)/shard_map/ppermute | solution.py:93
  255.6 2.0 shard_map.139
  (152 shorter events, 31.6 us)
Async XLA Ops:
  5.4 36.7 %collective-permute-start.9 = (bf16[48,128,128]{2,1,0:T(8,128)(2,1)}, bf16[48,128,128]{2,1,0:T(8,128)(2,1)S(1)}, u32[]{:S(2)}, u32[]{:S(2)}) collective-permute-start(bf16[48,128,128]{2,1,0:T(8,128)(2,1)} %pad_maximum_fusion), channel_id=1, source_target_pairs={{0,1},{1,0},{2,17},{3,16},{4,5},{5,4},{6,21},{7,20},{8,9},{9,8},{1... | collective-permute-start | bytes 4718600 | tf_op jit(solution)/shard_map/ppermute | solution.py:93
  12.0 45.5 %collective-permute-start.2 = (bf16[48,128,128]{2,1,0:T(8,128)(2,1)}, bf16[48,128,128]{2,1,0:T(8,128)(2,1)}, u32[]{:S(2)}, u32[]{:S(2)}) collective-permute-start(bf16[48,128,128]{2,1,0:T(8,128)(2,1)} %bitcast.34), channel_id=1, source_target_pairs={{0,1},{1,0},{2,17},{3,16},{4,5},{5,4},{6,21},{7,20},{8,9},{9,8},{1... | collective-permute-start | bytes 4718600 | tf_op jit(solution)/shard_map/ppermute | solution.py:93
  12.0 26.8 %collective-permute-start.15 = (bf16[24,128,128]{2,1,0:T(8,128)(2,1)}, bf16[24,128,128]{2,1,0:T(8,128)(2,1)S(1)}, u32[]{:S(2)}, u32[]{:S(2)}) collective-permute-start(bf16[24,128,128]{2,1,0:T(8,128)(2,1)} %bitcast.36), channel_id=1, source_target_pairs={{0,4},{1,5},{4,8},{5,9},{8,12},{9,13},{12,3},{13,2},{18,22},{19,23... | collective-permute-start | bytes 2359304 | tf_op jit(solution)/shard_map/ppermute | solution.py:93
  13.2 25.5 %collective-permute-start.21 = (bf16[24,128,128]{2,1,0:T(8,128)(2,1)}, bf16[24,128,128]{2,1,0:T(8,128)(2,1)S(1)}, u32[]{:S(2)}, u32[]{:S(2)}) collective-permute-start(bf16[24,128,128]{2,1,0:T(8,128)(2,1)} %bitcast.35), channel_id=1, source_target_pairs={{0,111},{1,110},{4,0},{5,1},{8,4},{9,5},{12,8},{13,9},{18,29},{19,... | collective-permute-start | bytes 2359304 | tf_op jit(solution)/shard_map/ppermute | solution.py:93
  15.2 40.4 %collective-permute-start = (bf16[24,128,128]{2,1,0:T(8,128)(2,1)S(1)}, bf16[24,128,128]{2,1,0:T(8,128)(2,1)S(1)}, u32[]{:S(2)}, u32[]{:S(2)}) collective-permute-start(bf16[24,128,128]{2,1,0:T(8,128)(2,1)S(1)} %constant_dynamic-slice_fusion), channel_id=1, source_target_pairs={{0,4},{1,110},{4,8},{5,1},{8,12},{9,5},{12,3},{13,9},{18,29},{19,2... | collective-permute-start | bytes 2359304 | tf_op jit(solution)/shard_map/ppermute | solution.py:93
  38.7 27.9 %collective-permute-start.16 = (bf16[24,128,128]{2,1,0:T(8,128)(2,1)S(1)}, bf16[24,128,128]{2,1,0:T(8,128)(2,1)S(1)}, u32[]{:S(2)}, u32[]{:S(2)}) collective-permute-start(bf16[24,128,128]{2,1,0:T(8,128)(2,1)S(1)} %collective-permute-done.15.refs_10_), channel_id=1, source_target_pairs={{0,16},{1,17},{2,18},{3,19},{4,20},{5,21},{6,22},{7,23},{8,24},{9,... | collective-permute-start | bytes 2359304 | tf_op jit(solution)/shard_map/ppermute | solution.py:93
  38.8 33.0 %collective-permute-start.22 = (bf16[24,128,128]{2,1,0:T(8,128)(2,1)S(1)}, bf16[24,128,128]{2,1,0:T(8,128)(2,1)}, u32[]{:S(2)}, u32[]{:S(2)}) collective-permute-start(bf16[24,128,128]{2,1,0:T(8,128)(2,1)S(1)} %collective-permute-done.21.refs_16_), channel_id=1, source_target_pairs={{0,16},{1,17},{2,18},{3,19},{4,20},{5,21},{6,22},{7,23},{8,24},{9,... | collective-permute-start | bytes 2359304 | tf_op jit(solution)/shard_map/ppermute | solution.py:93
  43.5 29.1 %collective-permute-start.17 = (bf16[24,128,128]{2,1,0:T(8,128)(2,1)}, bf16[24,128,128]{2,1,0:T(8,128)(2,1)}, u32[]{:S(2)}, u32[]{:S(2)}) collective-permute-start(bf16[24,128,128]{2,1,0:T(8,128)(2,1)} %get-tuple-element.54), channel_id=1, source_target_pairs={{0,4},{1,5},{2,6},{3,7},{4,8},{5,9},{6,10},{7,11},{8,12},{9,13},{1... | collective-permute-start | bytes 2359304 | tf_op jit(solution)/shard_map/ppermute | solution.py:93
  55.6 32.6 %collective-permute-start.23 = (bf16[24,128,128]{2,1,0:T(8,128)(2,1)}, bf16[24,128,128]{2,1,0:T(8,128)(2,1)}, u32[]{:S(2)}, u32[]{:S(2)}) collective-permute-start(bf16[24,128,128]{2,1,0:T(8,128)(2,1)} %get-tuple-element.53), channel_id=1, source_target_pairs={{0,111},{1,110},{2,13},{3,12},{4,0},{5,1},{6,2},{7,3},{8,4},{9,5},... | collective-permute-start | bytes 2359304 | tf_op jit(solution)/shard_map/ppermute | solution.py:93
  57.5 63.6 %collective-permute-start.12 = (bf16[48,128,128]{2,1,0:T(8,128)(2,1)S(1)}, bf16[48,128,128]{2,1,0:T(8,128)(2,1)}, u32[]{:S(2)}, u32[]{:S(2)}) collective-permute-start(bf16[48,128,128]{2,1,0:T(8,128)(2,1)S(1)} %collective-permute-done.9.refs_2_), channel_id=1, source_target_pairs={{2,3},{3,2},{6,7},{7,6},{10,11},{11,10},{14,15},{15,14},{16,17},{1... | collective-permute-start | bytes 4718600 | tf_op jit(solution)/shard_map/ppermute | solution.py:93
  67.6 72.9 %collective-permute-start.8 = (bf16[96,128,128]{2,1,0:T(8,128)(2,1)}, bf16[96,128,128]{2,1,0:T(8,128)(2,1)}, u32[]{:S(2)}, u32[]{:S(2)}) collective-permute-start(bf16[96,128,128]{2,1,0:T(8,128)(2,1)} %bitcast.33.refs_0_), channel_id=1, source_target_pairs={{0,16},{1,17},{4,20},{5,21},{8,24},{9,25},{12,28},{13,29},{18,2},{... | collective-permute-start | bytes 9437192 | tf_op jit(solution)/shard_map/ppermute | solution.py:93
  71.8 34.7 %collective-permute-start.3 = (bf16[24,128,128]{2,1,0:T(8,128)(2,1)}, bf16[24,128,128]{2,1,0:T(8,128)(2,1)S(1)}, u32[]{:S(2)}, u32[]{:S(2)}) collective-permute-start(bf16[24,128,128]{2,1,0:T(8,128)(2,1)} %get-tuple-element.50), channel_id=1, source_target_pairs={{0,4},{1,110},{2,13},{3,7},{4,8},{5,1},{6,2},{7,11},{8,12},{9,5},{... | collective-permute-start | bytes 2359304 | tf_op jit(solution)/shard_map/ppermute | solution.py:93
  72.6 33.9 %collective-permute-start.33 = (bf16[24,128,128]{2,1,0:T(8,128)(2,1)}, bf16[24,128,128]{2,1,0:T(8,128)(2,1)}, u32[]{:S(2)}, u32[]{:S(2)}) collective-permute-start(bf16[24,128,128]{2,1,0:T(8,128)(2,1)} %get-tuple-element.50), channel_id=1, source_target_pairs={{0,111},{1,5},{2,6},{3,12},{4,0},{5,9},{6,10},{7,3},{8,4},{9,13},{... | collective-permute-start | bytes 2359304 | tf_op jit(solution)/shard_map/ppermute | solution.py:93
  88.2 32.6 %collective-permute-start.31 = (bf16[24,128,128]{2,1,0:T(8,128)(2,1)}, bf16[24,128,128]{2,1,0:T(8,128)(2,1)S(1)}, u32[]{:S(2)}, u32[]{:S(2)}) collective-permute-start(bf16[24,128,128]{2,1,0:T(8,128)(2,1)} %get-tuple-element.49), channel_id=1, source_target_pairs={{0,4},{1,110},{2,13},{3,7},{4,8},{5,1},{6,2},{7,11},{8,12},{9,5},{... | collective-permute-start | bytes 2359304 | tf_op jit(solution)/shard_map/ppermute | solution.py:93
  106.4 21.5 %collective-permute-start.10 = (bf16[48,128,128]{2,1,0:T(8,128)(2,1)S(1)}, bf16[48,128,128]{2,1,0:T(8,128)(2,1)}, u32[]{:S(2)}, u32[]{:S(2)}) collective-permute-start(bf16[48,128,128]{2,1,0:T(8,128)(2,1)S(1)} %collective-permute-done.9.refs_2_), channel_id=1, source_target_pairs={{0,16},{1,17},{2,18},{3,19},{4,20},{5,21},{6,22},{7,23},{8,24},{9,... | collective-permute-start | bytes 4718600 | tf_op jit(solution)/shard_map/ppermute | solution.py:93
  106.5 26.5 %collective-permute-start.5 = (bf16[48,128,128]{2,1,0:T(8,128)(2,1)}, bf16[48,128,128]{2,1,0:T(8,128)(2,1)}, u32[]{:S(2)}, u32[]{:S(2)}) collective-permute-start(bf16[48,128,128]{2,1,0:T(8,128)(2,1)} %collective-permute-done.2.refs_4_), channel_id=1, source_target_pairs={{2,3},{3,2},{6,7},{7,6},{10,11},{11,10},{14,15},{15,14},{16,17},{1... | collective-permute-start | bytes 4718600 | tf_op jit(solution)/shard_map/ppermute | solution.py:93
  126.8 21.4 %collective-permute-start.34 = (bf16[24,128,128]{2,1,0:T(8,128)(2,1)}, bf16[24,128,128]{2,1,0:T(8,128)(2,1)S(1)}, u32[]{:S(2)}, u32[]{:S(2)}) collective-permute-start(bf16[24,128,128]{2,1,0:T(8,128)(2,1)} %collective-permute-done.33), channel_id=1, source_target_pairs={{0,1},{1,0},{2,3},{3,2},{4,5},{5,4},{6,7},{7,6},{8,9},{9,8},{10,11... | collective-permute-start | bytes 2359304 | tf_op jit(solution)/shard_map/ppermute | solution.py:93
  127.9 22.5 %collective-permute-start.19 = (bf16[24,128,128]{2,1,0:T(8,128)(2,1)S(1)}, bf16[24,128,128]{2,1,0:T(8,128)(2,1)}, u32[]{:S(2)}, u32[]{:S(2)}) collective-permute-start(bf16[24,128,128]{2,1,0:T(8,128)(2,1)S(1)} %get-tuple-element.52), channel_id=1, source_target_pairs={{2,6},{3,7},{6,10},{7,11},{10,14},{11,15},{14,33},{15,32},{16,20},... | collective-permute-start | bytes 2359304 | tf_op jit(solution)/shard_map/ppermute | solution.py:93
  138.1 29.7 %collective-permute-start.13 = (bf16[48,128,128]{2,1,0:T(8,128)(2,1)}, bf16[48,128,128]{2,1,0:T(8,128)(2,1)}, u32[]{:S(2)}, u32[]{:S(2)}) collective-permute-start(bf16[48,128,128]{2,1,0:T(8,128)(2,1)} %collective-permute-done.12.refs_6_), channel_id=1, source_target_pairs={{2,18},{3,19},{6,22},{7,23},{10,26},{11,27},{14,30},{15,31},{16,0}... | collective-permute-start | bytes 4718600 | tf_op jit(solution)/shard_map/ppermute | solution.py:93
  140.5 27.3 %collective-permute-start.14 = (bf16[48,128,128]{2,1,0:T(8,128)(2,1)}, bf16[48,128,128]{2,1,0:T(8,128)(2,1)}, u32[]{:S(2)}, u32[]{:S(2)}) collective-permute-start(bf16[48,128,128]{2,1,0:T(8,128)(2,1)} %collective-permute-done.5.refs_8_), channel_id=1, source_target_pairs={{2,18},{3,19},{6,22},{7,23},{10,26},{11,27},{14,30},{15,31},{16,0}... | collective-permute-start | bytes 4718600 | tf_op jit(solution)/shard_map/ppermute | solution.py:93
  158.7 37.2 %collective-permute-start.1 = (bf16[24,128,128]{2,1,0:T(8,128)(2,1)}, bf16[24,128,128]{2,1,0:T(8,128)(2,1)S(1)}, u32[]{:S(2)}, u32[]{:S(2)}) collective-permute-start(bf16[24,128,128]{2,1,0:T(8,128)(2,1)} %copy-done.1), channel_id=1, source_target_pairs={{0,16},{1,17},{2,18},{3,19},{4,20},{5,21},{6,22},{7,23},{8,24},{9,... | collective-permute-start | bytes 2359304 | tf_op jit(solution)/shard_map/ppermute | solution.py:93
  167.2 28.7 %collective-permute-start.4 = (bf16[24,128,128]{2,1,0:T(8,128)(2,1)}, bf16[24,128,128]{2,1,0:T(8,128)(2,1)S(1)}, u32[]{:S(2)}, u32[]{:S(2)}) collective-permute-start(bf16[24,128,128]{2,1,0:T(8,128)(2,1)} %copy-done.3), channel_id=1, source_target_pairs={{0,16},{1,17},{2,18},{3,19},{4,20},{5,21},{6,22},{7,23},{8,24},{9,... | collective-permute-start | bytes 2359304 | tf_op jit(solution)/shard_map/ppermute | solution.py:93
  167.2 37.4 %collective-permute-start.32 = (bf16[24,128,128]{2,1,0:T(8,128)(2,1)S(1)}, bf16[24,128,128]{2,1,0:T(8,128)(2,1)S(1)}, u32[]{:S(2)}, u32[]{:S(2)}) collective-permute-start(bf16[24,128,128]{2,1,0:T(8,128)(2,1)S(1)} %collective-permute-done.31.refs_0_), channel_id=1, source_target_pairs={{0,16},{1,17},{2,18},{3,19},{4,20},{5,21},{6,22},{7,23},{8,24},{9,... | collective-permute-start | bytes 2359304 | tf_op jit(solution)/shard_map/ppermute | solution.py:93
  167.7 36.9 %collective-permute-start.35 = (bf16[24,128,128]{2,1,0:T(8,128)(2,1)S(1)}, bf16[24,128,128]{2,1,0:T(8,128)(2,1)S(1)}, u32[]{:S(2)}, u32[]{:S(2)}) collective-permute-start(bf16[24,128,128]{2,1,0:T(8,128)(2,1)S(1)} %collective-permute-done.34.refs_2_), channel_id=1, source_target_pairs={{0,16},{1,17},{2,18},{3,19},{4,20},{5,21},{6,22},{7,23},{8,24},{9,... | collective-permute-start | bytes 2359304 | tf_op jit(solution)/shard_map/ppermute | solution.py:93
  167.8 28.1 %collective-permute-start.7 = (bf16[24,128,128]{2,1,0:T(8,128)(2,1)}, bf16[24,128,128]{2,1,0:T(8,128)(2,1)S(1)}, u32[]{:S(2)}, u32[]{:S(2)}) collective-permute-start(bf16[24,128,128]{2,1,0:T(8,128)(2,1)} %collective-permute-done.6.refs_4_), channel_id=1, source_target_pairs={{0,16},{1,17},{2,18},{3,19},{4,20},{5,21},{6,22},{7,23},{8,24},{9,... | collective-permute-start | bytes 2359304 | tf_op jit(solution)/shard_map/ppermute | solution.py:93
  210.3 22.9 %collective-permute-start.36 = (bf16[24,128,128]{2,1,0:T(8,128)(2,1)S(1)}, bf16[24,128,128]{2,1,0:T(8,128)(2,1)S(1)}, u32[]{:S(2)}, u32[]{:S(2)}) collective-permute-start(bf16[24,128,128]{2,1,0:T(8,128)(2,1)S(1)} %get-tuple-element.37), channel_id=1, source_target_pairs={{0,0},{17,3},{3,16},{18,19},{4,4},{21,7},{7,20},{22,23},{8,8},{25,... | collective-permute-start | bytes 2359304 | tf_op jit(solution)/shard_map/ppermute | solution.py:93
  211.6 23.6 %collective-permute-start.37 = (bf16[24,128,128]{2,1,0:T(8,128)(2,1)S(1)}, bf16[24,128,128]{2,1,0:T(8,128)(2,1)S(1)}, u32[]{:S(2)}, u32[]{:S(2)}) collective-permute-start(bf16[24,128,128]{2,1,0:T(8,128)(2,1)S(1)} %get-tuple-element.38), channel_id=1, source_target_pairs={{0,1},{17,2},{3,17},{18,18},{4,5},{21,6},{7,21},{22,22},{8,9},{25,... | collective-permute-start | bytes 2359304 | tf_op jit(solution)/shard_map/ppermute | solution.py:93
  212.3 24.8 %collective-permute-start.38 = (bf16[24,128,128]{2,1,0:T(8,128)(2,1)S(1)}, bf16[24,128,128]{2,1,0:T(8,128)(2,1)S(1)}, u32[]{:S(2)}, u32[]{:S(2)}) collective-permute-start(bf16[24,128,128]{2,1,0:T(8,128)(2,1)S(1)} %get-tuple-element.39), channel_id=1, source_target_pairs={{0,2},{17,1},{3,18},{18,17},{4,6},{21,5},{7,22},{22,21},{8,10},{25... | collective-permute-start | bytes 2359304 | tf_op jit(solution)/shard_map/ppermute | solution.py:93
  213.0 32.2 %collective-permute-start.39 = (bf16[24,128,128]{2,1,0:T(8,128)(2,1)S(1)}, bf16[24,128,128]{2,1,0:T(8,128)(2,1)S(1)}, u32[]{:S(2)}, u32[]{:S(2)}) collective-permute-start(bf16[24,128,128]{2,1,0:T(8,128)(2,1)S(1)} %get-tuple-element.40), channel_id=1, source_target_pairs={{0,3},{17,0},{3,19},{18,16},{4,7},{21,4},{7,23},{22,20},{8,11},{25... | collective-permute-start | bytes 2359304 | tf_op jit(solution)/shard_map/ppermute | solution.py:93
  214.3 30.9 %collective-permute-start.27 = (bf16[24,128,128]{2,1,0:T(8,128)(2,1)S(1)}, bf16[24,128,128]{2,1,0:T(8,128)(2,1)S(1)}, u32[]{:S(2)}, u32[]{:S(2)}) collective-permute-start(bf16[24,128,128]{2,1,0:T(8,128)(2,1)S(1)} %get-tuple-element.31), channel_id=1, source_target_pairs={{16,1},{1,2},{19,17},{2,18},{20,5},{5,6},{23,21},{6,22},{24,9},{9,... | collective-permute-start | bytes 2359304 | tf_op jit(solution)/shard_map/ppermute | solution.py:93
  233.2 22.4 %collective-permute-start.28 = (bf16[24,128,128]{2,1,0:T(8,128)(2,1)S(1)}, bf16[24,128,128]{2,1,0:T(8,128)(2,1)S(1)}, u32[]{:S(2)}, u32[]{:S(2)}) collective-permute-start(bf16[24,128,128]{2,1,0:T(8,128)(2,1)S(1)} %get-tuple-element.32), channel_id=1, source_target_pairs={{16,0},{1,3},{19,16},{2,19},{20,4},{5,7},{23,20},{6,23},{24,8},{9,... | collective-permute-start | bytes 2359304 | tf_op jit(solution)/shard_map/ppermute | solution.py:93
  235.2 20.4 %collective-permute-start.29 = (bf16[24,128,128]{2,1,0:T(8,128)(2,1)S(1)}, bf16[24,128,128]{2,1,0:T(8,128)(2,1)S(1)}, u32[]{:S(2)}, u32[]{:S(2)}) collective-permute-start(bf16[24,128,128]{2,1,0:T(8,128)(2,1)S(1)} %get-tuple-element.33), channel_id=1, source_target_pairs={{16,3},{1,0},{19,19},{2,16},{20,7},{5,4},{23,23},{6,20},{24,11},{9... | collective-permute-start | bytes 2359304 | tf_op jit(solution)/shard_map/ppermute | solution.py:93
  (32 other events, 727.8 us)

commit v2 on v1

v2 whole, which is shorter than its diff:
```python
import jax
import jax.numpy as jnp
from jax import lax
from jax.experimental import pallas as pl
from jax.experimental.pallas import tpu as pltpu
from jax.sharding import PartitionSpec as P


AXES = ("row", "col", "layer")
B = 128
SLOTS = 24
TOTAL = 512
WIN = 28
BF = jnp.bfloat16
F32 = jnp.float32

RIGHT = 0
LEFT = RIGHT + WIN * WIN
KEPT = LEFT + 4 * WIN
PLACE = KEPT + 4 * SLOTS
FLAGS = PLACE + 1
ZERO = 384


def dev(z, c, y, x):
    return ((2 * z + c) * 4 + y) * 4 + x


def devices():
    return [(z, c, y, x) for z in range(4) for c in range(2) for y in range(4) for x in range(4)]


def is_home(c, x):
    return c == (1 if x >= 2 else 0)


def is_first(x):
    return x in (0, 3)


def after(z, c, y, x):
    if y < 3:
        return (z, c, y + 1, x)
    if x < 2:
        return (z, c, 0, 3 - x)
    return ((z + 1) % 4, c, 0, 3 - x)


def before(z, c, y, x):
    if y > 0:
        return (z, c, y - 1, x)
    if x >= 2:
        return (z, c, 3, 3 - x)
    return ((z - 1) % 4, c, 3, 3 - x)


PAIRS_SHARE = [
    (dev(z, c, y, x), dev(z, c, y, x ^ 1) if is_home(c, x) else dev(z, 1 - c, y, 3 - x))
    for z, c, y, x in devices()
]
PAIRS_PASS = [(dev(z, c, y, x), dev(z, c, y, x ^ 1)) for z, c, y, x in devices() if not is_home(c, x)]
PAIRS_WIDE = [(dev(*d), dev(*(after(*d) if is_first(d[3]) else before(*d)))) for d in devices()]
PAIRS_NARROW = [(dev(*d), dev(*(before(*d) if is_first(d[3]) else after(*d)))) for d in devices()]
PAIRS_RELAY = [(dev(z, c, y, x), dev(z, c, y, x ^ 1)) for z, c, y, x in devices()]
PAIRS_SWAP = [(dev(z, c, y, x), dev(z, 1 - c, y, x)) for z, c, y, x in devices()]
AT_HOME = {dev(z, c, y, x) for z, c, y, x in devices() if is_home(c, x)}


def from_home(pairs):
    return [p for p in pairs if p[0] in AT_HOME]


def from_guest(pairs):
    return [p for p in pairs if p[0] not in AT_HOME]


def reached(pairs, start):
    ends = {p[1] for p in pairs}
    return [p for p in start if p[0] in ends]


def turns(pair):
    return pair[0] % 4 != pair[1] % 4


def straight(pairs):
    ends = {dev(*d): d for d in devices()}
    out = []
    for a, b in pairs:
        z, c, y, x = ends[a]
        out.append((dev(z, 1 - c, y, 3 - x), b))
    return out


def only(pairs, home, turn):
    return [p for p in pairs if (p[0] in AT_HOME) == home and turns(p) == turn]


def over(pairs):
    return reached(pairs, PAIRS_SWAP)


OWN_WIDE = only(PAIRS_WIDE, True, False) + straight(only(PAIRS_WIDE, False, True))
OWN_WIDE2 = only(PAIRS_WIDE, True, True)
SHARED_WIDE = [p for p in PAIRS_WIDE if p[0] in AT_HOME or not turns(p)]
OWN_NARROW = only(PAIRS_NARROW, True, False)
OWN_NARROW2 = only(PAIRS_NARROW, True, True)
STRAIGHT = straight(only(PAIRS_NARROW, False, True))
SHARED_NARROW = from_home(PAIRS_NARROW)
GUEST_NARROW = only(PAIRS_NARROW, False, False)
PASSED_NARROW = from_guest(PAIRS_NARROW)
RELAY = reached(GUEST_NARROW, PAIRS_RELAY)
RELAY2 = reached(STRAIGHT, PAIRS_RELAY)


def pairs_out(k, places):
    pairs = []
    for z in range(4):
        for y in range(4):
            for t in range(2):
                for n in places:
                    chip = ((0, 1), (3, 2))[t][n // 2]
                    pairs.append((dev(z, n % 2, y, chip), dev(z, t, y, n ^ k)))
    return pairs


def send(value, pairs):
    return lax.ppermute(value, AXES, pairs)


class Loads:
    def __init__(self, dest, sems):
        self.dest, self.sems, self.waits = dest, sems, []

    def add(self, choices, at, size, gate=None):
        q = len(self.waits)

        def copy(src, first):
            return pltpu.make_async_copy(
                src.at[pl.ds(first, size)], self.dest.at[pl.ds(at, size)], self.sems.at[q]
            )

        for flag, src, first in choices:
            on = flag if gate is None else gate if flag is None else gate & flag
            if on is None:
                copy(src, first).start()
            else:
                pl.when(on)(lambda src=src, first=first: copy(src, first).start())
        self.waits.append((gate, copy(*choices[0][1:])))

    def wait(self):
        for gate, w in self.waits:
            if gate is None:
                w.wait()
            else:
                pl.when(gate)(w.wait)


def products(tab, left, raw, first, origins, put, after=None):
    def pair(p, carry):
        on = [jnp.where((2 * p + 13 >= o) & (2 * p <= o + 15), 1, 0) for o in origins]
        count = sum(on)
        lead = jnp.where(on[0] == 1, 0, jnp.where(on[1] == 1, 1, 2))
        if len(origins) == 4:
            lead = jnp.where(on[0] + on[1] + on[2] == 0, 3, lead)

        for groups in range(len(origins) + 1):

            @pl.when(count == groups)
            def _():
                if groups == 0:
                    put(2 * p, jnp.zeros((4 * B, B), F32))
                    put(2 * p + 1, jnp.zeros((4 * B, B), F32))
                    return
                lhs = left[:, pl.ds(pl.multiple_of(lead * 4 * B, 4 * B), groups * 4 * B)]
                rows = []
                for j in range(4 * groups):
                    at = RIGHT + (first + 4 * lead + j) * WIN + 2 * p
                    rows.append(jnp.concatenate([raw[tab[at]], raw[tab[at + 1]]], axis=1))
                r = jnp.dot(lhs, jnp.concatenate(rows, axis=0), preferred_element_type=F32)
                put(2 * p, r[:, :B])
                put(2 * p + 1, r[:, B:])

        if after is not None:
            after(p)
        return carry

    lax.fori_loop(0, WIN // 2, pair, 0)


def flags(tab, q, side):
    f = tab[FLAGS + q] if side == 0 else 1 - tab[FLAGS + q]
    return f == 1, f == 0


def first_kernel(tab, *refs):
    own, r, z = (refs[2 * q : 2 * q + 2] for q in range(3))
    acc, far, total, raw, left, sems, done = refs[6:]
    loads = Loads(raw, sems)
    for side in range(2):
        yes, no = flags(tab, 0, side)
        loads.add([(None, r[side], 0)], side * 96, 96)
        loads.add([(yes, own[side], 0), (no, z[side], 0)], (2 + side) * 96, 96)
    raw[ZERO] = jnp.zeros((B, B), BF)
    loads.wait()

    def one_row(i, carry):
        rows = pl.ds(pl.multiple_of(i * B, B), B)
        for j in range(WIN):
            block = raw[tab[LEFT + i * WIN + j]]
            if j < 16:
                left[rows, j * B : (j + 1) * B] = block
            else:
                far[rows, (j - 16) * B : (j - 15) * B] = block
        return carry

    lax.fori_loop(0, 4, one_row, 0)

    def put(c, value):
        total[c] = value

    def leave(p):
        two = pl.ds(2 * p, 2)
        return pltpu.make_async_copy(total.at[two], acc.at[two], done.at[p])

    base = 12 - 4 * tab[PLACE]
    products(tab, left, raw, 0, [base + 4 * g for g in range(4)], put, lambda p: leave(p).start())
    for p in range(WIN // 2):
        leave(p).wait()


def select(tab, total, outs):
    place = tab[PLACE]
    for k in range(4):
        lam = (place ^ k) * 6
        out = outs[k]

        def one_row(i, carry):
            for s in range(6):
                c = tab[KEPT + i * SLOTS + lam + s]
                out[i * 6 + s] = total[c, pl.ds(pl.multiple_of(i * B, B), B)].astype(BF)
            return carry

        lax.fori_loop(0, 4, one_row, 0)


def second_kernel(tab, *refs):
    own_w, own_w2, r_w, relay, relay2 = (refs[2 * q : 2 * q + 2] for q in range(5))
    own_n, own_n2, r_n, r_x, own_x, z_n = (refs[10 + 2 * q : 12 + 2 * q] for q in range(6))
    left, acc = refs[22:24]
    outs, raw, total, sems = refs[24:28], *refs[28:]
    loads = Loads(raw, sems)
    edge = (tab[PLACE] == 0) | (tab[PLACE] == 3)
    inside = jnp.logical_not(edge)
    one = tab[FLAGS + 5]
    for side in range(2):
        yes, no = flags(tab, 1, side)
        turn = tab[FLAGS + 3] == 1
        on = jnp.logical_not(turn)
        for first, size, gate in ((24 * one, 48, None), (48 - 48 * one, 24, edge)):
            loads.add(
                [(yes | on, r_w[side], first), (no & turn, own_w[side], first)],
                side * 72 + first, size, gate,
            )
            loads.add(
                [
                    (yes & on, own_w[side], first), (yes & turn, own_w2[side], first),
                    (no & on, relay[side], first), (no & turn, relay2[side], first),
                ],
                (2 + side) * 72 + first, size, gate,
            )
        yes, no = flags(tab, 2, side)
        turn = tab[FLAGS + 4] == 1
        on = jnp.logical_not(turn)
        first = 48 - 48 * one
        loads.add(
            [(yes, r_n[side], 0), (no & on, r_x[side], first), (no & turn, own_x[side], first)],
            288 + side * 24, 24, inside,
        )
        loads.add(
            [(yes & on, own_n[side], 0), (yes & turn, own_n2[side], 0), (no, z_n[side], 0)],
            288 + (2 + side) * 24, 24, inside,
        )
    raw[ZERO] = jnp.zeros((B, B), BF)
    loads.wait()

    def put(c, value):
        total[c] = acc[c] + value

    base = 12 - 4 * tab[PLACE]
    origins = [jnp.where(4 * g < base, 4 * g, 4 * g + 16) for g in range(3)]
    products(tab, left, raw, 16, origins, put)
    select(tab, total, outs)


def place_kernel(where, *refs):
    parts, out, sems = refs[:4], refs[4], refs[5]
    x = where[0]
    for n in range(4):
        for k in range(4):

            @pl.when((x ^ n) == k)
            def _():
                pltpu.make_async_copy(parts[k], out.at[pl.ds(24 * n, 24)], sems.at[n]).start()

    for n in range(4):
        pltpu.make_async_copy(parts[0], out.at[pl.ds(24 * n, 24)], sems.at[n]).wait()


ANY = pl.BlockSpec(memory_space=pl.ANY)
VM = pl.BlockSpec(memory_space=pltpu.VMEM)
ACC = jax.ShapeDtypeStruct((WIN, 4 * B, B), F32)
SIDE = jax.ShapeDtypeStruct((4 * B, 12 * B), BF)
OUT = jax.ShapeDtypeStruct((24, B, B), BF)


def call(body, tab, far, near, outs, scratch, vmem, flops, moved, leaves=0):
    single = not isinstance(outs, list)
    return pl.pallas_call(
        body,
        out_shape=outs,
        grid_spec=pltpu.PrefetchScalarGridSpec(
            num_scalar_prefetch=1,
            grid=(),
            in_specs=[ANY] * len(far) + [VM] * len(near),
            out_specs=VM if single else [ANY] * leaves + [VM] * (len(outs) - leaves),
            scratch_shapes=scratch,
        ),
        compiler_params=pltpu.CompilerParams(vmem_limit_bytes=vmem * 2**20),
        cost_estimate=pl.CostEstimate(flops=flops, transcendentals=0, bytes_accessed=moved),
    )(tab, *far, *near)


def sems(n):
    return pltpu.SemaphoreType.DMA((n,))


def tables(pattern, out_pattern):
    row = lax.axis_index("row")
    y = lax.axis_index("col")
    x = lax.axis_index("layer")
    c = row % 2
    first = jnp.logical_or(x == 0, x == 3)
    group = ((row // 2) * 2 + (x >= 2).astype(jnp.int32)) * 4 + y
    place = jnp.where(first, 0, 2) + c
    base = 16 * group + 4 * place - 12
    k = jnp.arange(12)
    r = jnp.concatenate([jnp.arange(16), jnp.where(k < 12 - 4 * place, k - 12, k + 4) + 4 * place])
    found = jnp.take(pattern, (16 * group + r) % TOTAL, axis=0)
    kept = jnp.take(out_pattern, (base + 12 + jnp.arange(4)) % TOTAL, axis=0)
    kept = (kept - base) % TOTAL

    def is_home_of(chip, core):
        return (core == (chip >= 2).astype(jnp.int32)).astype(jnp.int32)

    def held(chip):
        out = []
        for core in (c, 1 - c):
            home = is_home_of(chip, core) == 1
            out.append((jnp.where(home, chip ^ 1, 3 - chip), jnp.where(home, chip, (3 - chip) ^ 1)))
        return [out[0][0], out[1][0], out[0][1], out[1][1]]

    low = jnp.where(y == 0, 3 - x, x)
    high = jnp.where(y == 3, 3 - x, x)
    wide = jnp.where(first, low, high)
    narrow = jnp.where(first, high, low)
    lam = jnp.stack([jnp.stack(v) for v in (held(x), held(wide), held(narrow))])
    kind = jnp.sum(
        jnp.where(lam[:, None, :] == jnp.arange(4)[None, :, None], jnp.arange(4), 0), axis=-1
    )
    pack = jnp.where((r >= 0) & (r < 16), 0, jnp.where((r < 0) == first, 1, 2))
    top = jnp.where(pack == 0, 0, jnp.where(pack == 1, jnp.where(first, -12, 16), jnp.where(first, 16, -4)))
    start = jnp.where(pack == 2, 288, 0) + 6 * (r - top)
    step = jnp.where(pack == 0, 96, jnp.where(pack == 1, 72, 24))
    kinds = jnp.sum(
        jnp.where(pack[:, None, None] == jnp.arange(3)[None, :, None], kind[None], 0), axis=1
    )
    pos = start[:, None, None] + step[:, None, None] * kinds[:, :, None] + jnp.arange(6)
    pos = pos.reshape(WIN, SLOTS) - ZERO
    rel = (found - base) % TOTAL
    hit = rel[:, :, None] == jnp.arange(WIN)
    right = jnp.sum(jnp.where(hit, pos[:, :, None], 0), axis=1) + ZERO
    mine = lax.dynamic_slice_in_dim(rel, 4 * place, 4, 0)
    spot = lax.dynamic_slice_in_dim(pos, 4 * place, 4, 0)
    hit = mine[:, :, None] == (r - 4 * place + 12)
    left = jnp.sum(jnp.where(hit, spot[:, :, None], 0), axis=1) + ZERO
    turned = [(v != x).astype(jnp.int32) for v in (wide, narrow)]
    homes = [is_home_of(v, c) for v in (x, wide, narrow)]
    small = jnp.stack([place, *homes, *turned, first.astype(jnp.int32)])
    return jnp.concatenate(
        [right.reshape(-1), left.reshape(-1), kept.reshape(-1), small]
    ).astype(jnp.int32)


def square(blocks, pattern, out_pattern):
    x = lax.axis_index("layer")
    first = jnp.logical_or(x == 0, x == 3)
    tab = tables(pattern, out_pattern)
    own = blocks.reshape(96, B, B)

    def cut(a, at, size, behind=None):
        if behind is not None:
            at, _ = lax.optimization_barrier((at, behind))
        return lax.dynamic_slice_in_dim(a, at, size, 0)

    at_w, at_x, at_n = (jnp.where(first, p, q) for p, q in ((24, 0), (0, 24), (0, 72)))

    r = send(own, PAIRS_SHARE)
    mine_w = cut(own, at_w, 72)
    mine_n = cut(own, at_n, 24, mine_w)
    own_w = send(mine_w, OWN_WIDE)
    own_n = send(mine_n, OWN_NARROW)
    own_x = send(cut(own, at_x, 72, mine_n), STRAIGHT)
    own_s = send(own, from_home(PAIRS_SWAP))

    z = send(r, PAIRS_PASS)
    shared_x = cut(r, at_x, 72)
    r_x = send(shared_x, GUEST_NARROW)
    shared_w = cut(r, at_w, 72, shared_x)
    r_w = send(shared_w, SHARED_WIDE)
    r_n = send(cut(r, at_n, 24, shared_w), SHARED_NARROW)
    own_w2 = send(mine_w, OWN_WIDE2)
    own_n2 = send(mine_n, OWN_NARROW2)
    r_s = send(r, PAIRS_SWAP)
    own_w_s = send(own_w, over(OWN_WIDE))
    own_n_s = send(own_n, over(OWN_NARROW))
    own_x_s = send(own_x, over(STRAIGHT))

    z_s = send(z, from_guest(PAIRS_SWAP))
    relay = send(r_x, RELAY)
    relay2 = send(own_x, RELAY2)
    z_n = send(cut(z, at_n, 24), PASSED_NARROW)
    r_x_s = send(r_x, over(GUEST_NARROW))

    r_n_s = send(r_n, over(SHARED_NARROW))
    own_n2_s = send(own_n2, over(OWN_NARROW2))
    relay2_s = send(relay2, over(RELAY2))
    z_n_s = send(z_n, over(PASSED_NARROW))
    r_w_s = send(r_w, over(SHARED_WIDE))
    own_w2_s = send(own_w2, over(OWN_WIDE2))
    relay_s = send(relay, over(RELAY))

    acc, far = call(
        first_kernel, tab, [own, own_s, r, r_s, z, z_s], [], [ACC, SIDE],
        [
            pltpu.VMEM((WIN, 4 * B, B), F32), pltpu.VMEM((ZERO + 1, B, B), BF),
            pltpu.VMEM((4 * B, 16 * B), BF), sems(4), sems(WIN // 2),
        ],
        32, 8 * 10**9, 22 * 10**6, 1,
    )
    more = [own_w, own_w_s, own_w2, own_w2_s, r_w, r_w_s, relay, relay_s, relay2, relay2_s]
    more += [own_n, own_n_s, own_n2, own_n2_s, r_n, r_n_s, r_x, r_x_s, own_x, own_x_s, z_n, z_n_s]
    ready = call(
        second_kernel, tab, more, [far, acc], [OUT] * 4,
        [pltpu.VMEM((ZERO + 1, B, B), BF), pltpu.VMEM((WIN, 4 * B, B), F32), sems(12)],
        36, 6 * 10**9, 22 * 10**6,
    )
    parts = [send(v, pairs_out(k, range(4))) for k, v in enumerate(ready)]
    out = call(
        place_kernel, x.reshape(1).astype(jnp.int32), parts, [],
        jax.ShapeDtypeStruct((96, B, B), BF), [sems(4)], 8, 0, 6 * 10**6,
    )
    return out.reshape(16, 6, B, B)


def solution(mesh):
    in_specs = (P(("row", "col"), "layer", None, None), P(), P())
    out_specs = P(("row", "col"), "layer", None, None)
    return jax.shard_map(square, mesh=mesh, in_specs=in_specs, out_specs=out_specs, check_vma=False)
```

time: 258 us -> 250 us (0.969)
  starting transfers between devices: 86.9 us -> 106 us
  waiting for transfers between devices: 103 us -> 88.9 us
  Pallas kernels: 37.4 us -> 32.4 us
  local copies, waits for them, and re-layouts: 25.8 us -> 21 us
    ppermute x40 -> x31, starting transfers between devices: 86.9 us -> 106 us  [send(): return lax.ppermute(value, AXES, pairs)]
    ppermute x40 -> x31, waiting for transfers between devices: 103 us -> 88.9 us  [send(): return lax.ppermute(value, AXES, pairs)]
    dynamic_slice x4 -> x10, local copies, waits for them, and re-layouts: 6.05 us -> 16.4 us  [the longest x7 16.3 us: cut(): return lax.dynamic_slice_in_dim(a, at, size, 0)]
    slice x4 -> x0, local copies, waits for them, and re-layouts: 8.35 us -> none  [the longest x1 2.73 us: square(): rb = send(own[24:72], PAIRS_SHARE)]
    unnamed x50 -> x20, local copies, waits for them, and re-layouts: 8.62 us -> 2.92 us
    pallas_call x4 -> x3, Pallas kernels: 37.4 us -> 32.4 us  [call(): pl.pallas_call(body, out_shape=outs, grid_spec=pltpu.PrefetchScalarGridSp...]
    concatenate x1, other arithmetic: 2.68 us -> 0.01 us  [tables(): jnp.concatenate([jnp.arange(16), jnp.where(k < 12 - 4 * place, k - 12, k...]
  transfers between devices with their start and end apart: 40 -> 31, of which waited for: 13 -> 7; matrix products, arithmetic and copies ran while one was open for 6% -> 8% of each run, Pallas kernels for 12% -> 7%
where the time goes in v2:
time: 250 us
  starting transfers between devices  106 us (42%)
  waiting for transfers between devices  88.9 us (36%)
  Pallas kernels  32.4 us (13%)
  local copies, waits for them, and re-layouts  21 us (8%)
    ppermute x31, starting transfers between devices, send(): return lax.ppermute(value, AXES, pairs)  106 us
    ppermute x31, waiting for transfers between devices, send(): return lax.ppermute(value, AXES, pairs)  88.9 us
    pallas_call x3, Pallas kernels, call(): pl.pallas_call(body, out_shape=outs, grid_spec=pltpu.PrefetchScalarGridSp...  32.4 us
    dynamic_slice x7, local copies, waits for them, and re-layouts, cut(): return lax.dynamic_slice_in_dim(a, at, size, 0)  16.3 us
  transfers between devices with their start and end apart: 31, of which 7 were waited for; matrix products, arithmetic and copies ran while one was open for 8% of the time, Pallas kernels for 7%

profile of v2, /device:TPU:1, one launch (start us, length us, event | category | flops | bytes accessed | tf_op | source)
XLA Modules:
  0.0 249.7 jit_solution(11752139130161235495)
XLA Ops:
  0.0 3.9 %collective-permute-start.4 = (bf16[96,128,128]{2,1,0:T(8,128)(2,1)}, bf16[96,128,128]{2,1,0:T(8,128)(2,1)}, u32[]{:S(2)}, u32[]{:S(2)}) collective-permute-start(bf16[96,128,128]{2,1,0:T(8,128)(2,1)} %bitcast.36), channel_id=1, source_target_pairs={{0,1},{1,0},{2,17},{3,16},{4,5},{5,4},{6,21},{7,20},{8,9},{9,8},{1... | collective-permute-start | bytes 9437192 | tf_op jit(solution)/shard_map/ppermute | solution.py:128
  3.9 3.5 %constant_dynamic-slice_fusion.6 = bf16[72,128,128]{2,1,0:T(8,128)(2,1)} fusion(bf16[96,128,128]{2,1,0:T(8,128)(2,1)} %bitcast.37, s32[]{:T(128)S(6)} %select_n.339), kind=kLoop, calls=%fused_computation.26 | loop fusion | bytes 4718596 | tf_op jit(solution)/shard_map/dynamic_slice | solution.py:404
  12.8 1.7 constant_dynamic-slice_fusion.2
  14.5 13.9 %collective-permute-start.10 = (bf16[72,128,128]{2,1,0:T(8,128)(2,1)}, bf16[72,128,128]{2,1,0:T(8,128)(2,1)}, u32[]{:S(2)}, u32[]{:S(2)}) collective-permute-start(bf16[72,128,128]{2,1,0:T(8,128)(2,1)} %constant_dynamic-slice_fusion.2), channel_id=1, source_target_pairs={{16,12},{29,33},{3,127},{14,18},{48,44},{61,65},{35,31},{46,50},{8... | collective-permute-start | bytes 7077896 | tf_op jit(solution)/shard_map/ppermute | solution.py:128
  29.7 2.1 collective-permute-start
  33.9 13.9 %collective-permute-done.4.refs_2_ = bf16[96,128,128]{2,1,0:T(8,128)(2,1)} collective-permute-done((bf16[96,128,128]{2,1,0:T(8,128)(2,1)}, bf16[96,128,128]{2,1,0:T(8,128)(2,1)}, u32[]{:S(2)}, u32[]{:S(2)}) %collective-permute-start.4) | collective-permute-done | bytes 3145760 | tf_op jit(solution)/shard_map/ppermute | solution.py:128
  49.4 3.4 %constant_dynamic-slice_fusion.5 = bf16[72,128,128]{2,1,0:T(8,128)(2,1)} fusion(bf16[96,128,128]{2,1,0:T(8,128)(2,1)} %collective-permute-done.4.refs_2_, s32[]{:T(128)S(6)} %select_n.340), kind=kLoop, calls=%fused_computation.25 | loop fusion | bytes 4718596 | tf_op jit(solution)/shard_map/dynamic_slice | solution.py:404
  52.8 3.4 %constant_dynamic-slice_fusion.4 = bf16[72,128,128]{2,1,0:T(8,128)(2,1)} fusion(bf16[96,128,128]{2,1,0:T(8,128)(2,1)} %collective-permute-done.4.refs_2_, s32[]{:T(128)S(6)} %select_n.341), kind=kLoop, calls=%fused_computation.24 | loop fusion | bytes 4718596 | tf_op jit(solution)/shard_map/dynamic_slice | solution.py:404
  58.1 2.1 collective-permute-start.11
  62.4 2.0 collective-permute-start.20
  64.4 6.0 %collective-permute-done.2.refs_2_ = bf16[72,128,128]{2,1,0:T(8,128)(2,1)} collective-permute-done((bf16[72,128,128]{2,1,0:T(8,128)(2,1)}, bf16[72,128,128]{2,1,0:T(8,128)(2,1)}, u32[]{:S(2)}, u32[]{:S(2)}) %collective-permute-start.2) | collective-permute-done | bytes 2359328 | tf_op jit(solution)/shard_map/ppermute | solution.py:128
  70.4 21.0 %collective-permute-start.21 = (bf16[96,128,128]{2,1,0:T(8,128)(2,1)}, bf16[96,128,128]{2,1,0:T(8,128)(2,1)}, u32[]{:S(2)}, u32[]{:S(2)}) collective-permute-start(bf16[96,128,128]{2,1,0:T(8,128)(2,1)} %collective-permute-done.4.refs_2_), channel_id=1, source_target_pairs={{2,3},{3,2},{6,7},{7,6},{10,11},{11,10},{14,15},{15,14},{16,17},{1... | collective-permute-start | bytes 9437192 | tf_op jit(solution)/shard_map/ppermute | solution.py:128
  95.0 13.1 %collective-permute-start.3 = (bf16[72,128,128]{2,1,0:T(8,128)(2,1)}, bf16[72,128,128]{2,1,0:T(8,128)(2,1)}, u32[]{:S(2)}, u32[]{:S(2)}) collective-permute-start(bf16[72,128,128]{2,1,0:T(8,128)(2,1)} %collective-permute-done.2.refs_2_), channel_id=1, source_target_pairs={{3,19},{14,30},{16,0},{29,13},{35,51},{46,62},{48,32},{61,45},{67,... | collective-permute-start | bytes 7077896 | tf_op jit(solution)/shard_map/ppermute | solution.py:128
  108.2 1.9 collective-permute-start.5
  110.2 13.4 %collective-permute-done.7.refs_16_ = bf16[72,128,128]{2,1,0:T(8,128)(2,1)} collective-permute-done((bf16[72,128,128]{2,1,0:T(8,128)(2,1)}, bf16[72,128,128]{2,1,0:T(8,128)(2,1)}, u32[]{:S(2)}, u32[]{:S(2)}) %collective-permute-start.7) | collective-permute-done | bytes 2359328 | tf_op jit(solution)/shard_map/ppermute | solution.py:128
  123.5 2.8 %collective-permute-start.8 = (bf16[72,128,128]{2,1,0:T(8,128)(2,1)}, bf16[72,128,128]{2,1,0:T(8,128)(2,1)}, u32[]{:S(2)}, u32[]{:S(2)}) collective-permute-start(bf16[72,128,128]{2,1,0:T(8,128)(2,1)} %collective-permute-done.7.refs_16_), channel_id=1, source_target_pairs={{3,2},{6,7},{7,6},{10,11},{11,10},{14,15},{16,17},{20,21},{21,20},... | collective-permute-start | bytes 7077896 | tf_op jit(solution)/shard_map/ppermute | solution.py:128
  127.1 3.0 %collective-permute-start.26 = (bf16[96,128,128]{2,1,0:T(8,128)(2,1)}, bf16[96,128,128]{2,1,0:T(8,128)(2,1)}, u32[]{:S(2)}, u32[]{:S(2)}) collective-permute-start(bf16[96,128,128]{2,1,0:T(8,128)(2,1)} %collective-permute-done.21.refs_4_), channel_id=1, source_target_pairs={{2,18},{3,19},{6,22},{7,23},{10,26},{11,27},{14,30},{15,31},{16,0}... | collective-permute-start | bytes 9437192 | tf_op jit(solution)/shard_map/ppermute | solution.py:128
  130.2 2.1 constant_dynamic-slice_fusion
  132.3 1.9 collective-permute-start.22
  135.3 26.1 %collective-permute-done.5.refs_4_ = bf16[72,128,128]{2,1,0:T(8,128)(2,1)} collective-permute-done((bf16[72,128,128]{2,1,0:T(8,128)(2,1)}, bf16[72,128,128]{2,1,0:T(8,128)(2,1)}, u32[]{:S(2)}, u32[]{:S(2)}) %collective-permute-start.5) | collective-permute-done | bytes 2359328 | tf_op jit(solution)/shard_map/ppermute | solution.py:128
  162.8 5.8 %collective-permute-start.19 = (bf16[72,128,128]{2,1,0:T(8,128)(2,1)}, bf16[72,128,128]{2,1,0:T(8,128)(2,1)}, u32[]{:S(2)}, u32[]{:S(2)}) collective-permute-start(bf16[72,128,128]{2,1,0:T(8,128)(2,1)} %collective-permute-done.7.refs_16_), channel_id=1, source_target_pairs={{3,19},{6,22},{7,23},{10,26},{11,27},{14,30},{16,0},{20,4},{21,5},... | collective-permute-start | bytes 7077896 | tf_op jit(solution)/shard_map/ppermute | solution.py:128
  168.5 2.7 %collective-permute-start.6 = (bf16[72,128,128]{2,1,0:T(8,128)(2,1)}, bf16[72,128,128]{2,1,0:T(8,128)(2,1)}, u32[]{:S(2)}, u32[]{:S(2)}) collective-permute-start(bf16[72,128,128]{2,1,0:T(8,128)(2,1)} %collective-permute-done.5.refs_4_), channel_id=1, source_target_pairs={{1,17},{2,18},{3,19},{4,20},{5,21},{6,22},{7,23},{8,24},{9,25},{10... | collective-permute-start | bytes 7077896 | tf_op jit(solution)/shard_map/ppermute | solution.py:128
  171.3 2.0 collective-permute-start.9
  174.9 2.2 collective-permute-start.23
  177.4 16.6 %shard_map.37 = (f32[28,512,128]{2,1,0:T(8,128)}, bf16[512,1536]{1,0:T(8,128)(2,1)S(1)}) custom-call(s32[999]{0:T(1024)S(1)} %concatenate.53.tab, bf16[96,128,128]{2,1,0:T(8,128)(2,1)S(1)} %bitcast.41, bf16[96,128,128]{2,1,0:T(8,128)(2,1)} %collective-permute-done.24.refs_1_, bf16[96,128,128]{2,1,0:T(8,128)(2,1)} %collective-permute-done.4.refs_2_, ...), custom_call_target="tpu_custom_call" | custom-call | flops 8000000000 | bytes 22000000 | tf_op jit(solution)/shard_map/pallas_call | solution.py:319
  194.1 13.8 %shard_map.38 = (bf16[24,128,128]{2,1,0:T(8,128)(2,1)S(1)}, bf16[24,128,128]{2,1,0:T(8,128)(2,1)S(1)}, bf16[24,128,128]{2,1,0:T(8,128)(2,1)S(1)}, bf16[24,128,128]{2,1,0:T(8,128)(2,1)S(1)}) custom-call(s32[999]{0:T(1024)S(1)} %concatenate.53.tab, bf16[72,128,128]{2,1,0:T(8,128)(2,1)} %collective-permute-done.refs_0_, ...), custom_call_target="tpu_custom_call" | custom-call | flops 6000000000 | bytes 22000000 | tf_op jit(solution)/shard_map/pallas_call | solution.py:319
  207.9 1.9 collective-permute-start.27
  209.8 1.9 collective-permute-start.28
  211.7 4.9 %collective-permute-start.29 = (bf16[24,128,128]{2,1,0:T(8,128)(2,1)S(1)}, bf16[24,128,128]{2,1,0:T(8,128)(2,1)S(1)}, u32[]{:S(2)}, u32[]{:S(2)}) collective-permute-start(bf16[24,128,128]{2,1,0:T(8,128)(2,1)S(1)} %get-tuple-element.23), channel_id=1, source_target_pairs={{0,2},{16,3},{1,0},{17,1},{3,18},{19,19},{2,16},{18,17},{4,6},{20,... | collective-permute-start | bytes 2359304 | tf_op jit(solution)/shard_map/ppermute | solution.py:128
  216.6 2.2 collective-permute-start.30
  218.8 27.5 %collective-permute-done.27.refs_0_ = bf16[24,128,128]{2,1,0:T(8,128)(2,1)S(1)} collective-permute-done((bf16[24,128,128]{2,1,0:T(8,128)(2,1)S(1)}, bf16[24,128,128]{2,1,0:T(8,128)(2,1)S(1)}, u32[]{:S(2)}, u32[]{:S(2)}) %collective-permute-start.27) | collective-permute-done | bytes 786464 | tf_op jit(solution)/shard_map/ppermute | solution.py:128
  247.7 2.0 shard_map.39
  (102 shorter events, 24.6 us)
Async XLA Ops:
  0.0 47.8 %collective-permute-start.4 = (bf16[96,128,128]{2,1,0:T(8,128)(2,1)}, bf16[96,128,128]{2,1,0:T(8,128)(2,1)}, u32[]{:S(2)}, u32[]{:S(2)}) collective-permute-start(bf16[96,128,128]{2,1,0:T(8,128)(2,1)} %bitcast.36), channel_id=1, source_target_pairs={{0,1},{1,0},{2,17},{3,16},{4,5},{5,4},{6,21},{7,20},{8,9},{9,8},{1... | collective-permute-start | bytes 9437192 | tf_op jit(solution)/shard_map/ppermute | solution.py:128
  8.4 3.1 %collective-permute-start.13 = (bf16[24,128,128]{2,1,0:T(8,128)(2,1)}, bf16[24,128,128]{2,1,0:T(8,128)(2,1)}, u32[]{:S(2)}, u32[]{:S(2)}) collective-permute-start(bf16[24,128,128]{2,1,0:T(8,128)(2,1)} %constant_dynamic-slice_fusion.3), channel_id=1, source_target_pairs={{1,5},{4,0},{5,9},{8,4},{9,13},{12,8},{18,22},{22,26},{23,19},{26,... | collective-permute-start | bytes 2359304 | tf_op jit(solution)/shard_map/ppermute | solution.py:128
  10.0 19.7 %collective-permute-start.15 = (bf16[24,128,128]{2,1,0:T(8,128)(2,1)}, bf16[24,128,128]{2,1,0:T(8,128)(2,1)}, u32[]{:S(2)}, u32[]{:S(2)}) collective-permute-start(bf16[24,128,128]{2,1,0:T(8,128)(2,1)} %constant_dynamic-slice_fusion.3), channel_id=1, source_target_pairs={{0,111},{13,2},{19,28},{30,49},{32,15},{45,34},{51,60},{62,81},{64... | collective-permute-start | bytes 2359304 | tf_op jit(solution)/shard_map/ppermute | solution.py:128
  11.5 20.3 %collective-permute-start.14 = (bf16[24,128,128]{2,1,0:T(8,128)(2,1)}, bf16[24,128,128]{2,1,0:T(8,128)(2,1)S(1)}, u32[]{:S(2)}, u32[]{:S(2)}) collective-permute-start(bf16[24,128,128]{2,1,0:T(8,128)(2,1)} %collective-permute-done.13.refs_10_), channel_id=1, source_target_pairs={{0,16},{4,20},{5,21},{8,24},{9,25},{13,29},{19,3},{22,6},{23,7},{2... | collective-permute-start | bytes 2359304 | tf_op jit(solution)/shard_map/ppermute | solution.py:128
  14.5 43.6 %collective-permute-start.10 = (bf16[72,128,128]{2,1,0:T(8,128)(2,1)}, bf16[72,128,128]{2,1,0:T(8,128)(2,1)}, u32[]{:S(2)}, u32[]{:S(2)}) collective-permute-start(bf16[72,128,128]{2,1,0:T(8,128)(2,1)} %constant_dynamic-slice_fusion.2), channel_id=1, source_target_pairs={{16,12},{29,33},{3,127},{14,18},{48,44},{61,65},{35,31},{46,50},{8... | collective-permute-start | bytes 7077896 | tf_op jit(solution)/shard_map/ppermute | solution.py:128
  28.4 63.1 %collective-permute-start.24 = (bf16[96,128,128]{2,1,0:T(8,128)(2,1)S(1)}, bf16[96,128,128]{2,1,0:T(8,128)(2,1)}, u32[]{:S(2)}, u32[]{:S(2)}) collective-permute-start(bf16[96,128,128]{2,1,0:T(8,128)(2,1)S(1)} %bitcast.40), channel_id=1, source_target_pairs={{0,16},{1,17},{4,20},{5,21},{8,24},{9,25},{12,28},{13,29},{18,2},{... | collective-permute-start | bytes 9437192 | tf_op jit(solution)/shard_map/ppermute | solution.py:128
  29.7 32.7 %collective-permute-start = (bf16[72,128,128]{2,1,0:T(8,128)(2,1)}, bf16[72,128,128]{2,1,0:T(8,128)(2,1)}, u32[]{:S(2)}, u32[]{:S(2)}) collective-permute-start(bf16[72,128,128]{2,1,0:T(8,128)(2,1)} %constant_dynamic-slice_fusion.6), channel_id=1, source_target_pairs={{0,4},{4,8},{5,1},{8,12},{9,5},{13,9},{19,23},{22,18},{23,27},{26,... | collective-permute-start | bytes 7077896 | tf_op jit(solution)/shard_map/ppermute | solution.py:128
  32.6 37.8 %collective-permute-start.2 = (bf16[72,128,128]{2,1,0:T(8,128)(2,1)}, bf16[72,128,128]{2,1,0:T(8,128)(2,1)}, u32[]{:S(2)}, u32[]{:S(2)}) collective-permute-start(bf16[72,128,128]{2,1,0:T(8,128)(2,1)} %constant_dynamic-slice_fusion.6), channel_id=1, source_target_pairs={{1,110},{12,3},{18,29},{31,48},{33,14},{44,35},{50,61},{63,80},{65... | collective-permute-start | bytes 7077896 | tf_op jit(solution)/shard_map/ppermute | solution.py:128
  47.8 9.6 %collective-permute-start.16 = (bf16[24,128,128]{2,1,0:T(8,128)(2,1)}, bf16[24,128,128]{2,1,0:T(8,128)(2,1)}, u32[]{:S(2)}, u32[]{:S(2)}) collective-permute-start(bf16[24,128,128]{2,1,0:T(8,128)(2,1)} %collective-permute-done.15.refs_12_), channel_id=1, source_target_pairs={{2,18},{15,31},{17,1},{28,12},{34,50},{47,63},{49,33},{60,44},{66,... | collective-permute-start | bytes 2359304 | tf_op jit(solution)/shard_map/ppermute | solution.py:128
  56.2 117.3 %copy-start.8 = (s32[512,24]{0,1:T(8,128)S(1)}, s32[512,24]{0,1:T(8,128)}, u32[]{:S(2)}) copy-start(s32[512,24]{0,1:T(8,128)} %param.4) | copy-start | bytes 147460
  57.4 2.8 %collective-permute-start.17 = (bf16[24,128,128]{2,1,0:T(8,128)(2,1)S(1)}, bf16[24,128,128]{2,1,0:T(8,128)(2,1)S(1)}, u32[]{:S(2)}, u32[]{:S(2)}) collective-permute-start(bf16[24,128,128]{2,1,0:T(8,128)(2,1)S(1)} %constant_dynamic-slice_fusion.1), channel_id=1, source_target_pairs={{0,111},{1,5},{4,0},{5,9},{8,4},{9,13},{12,8},{13,2},{18,22},{19,2... | collective-permute-start | bytes 2359304 | tf_op jit(solution)/shard_map/ppermute | solution.py:128
  58.1 36.8 %collective-permute-start.11 = (bf16[72,128,128]{2,1,0:T(8,128)(2,1)}, bf16[72,128,128]{2,1,0:T(8,128)(2,1)}, u32[]{:S(2)}, u32[]{:S(2)}) collective-permute-start(bf16[72,128,128]{2,1,0:T(8,128)(2,1)} %collective-permute-done.10.refs_18_), channel_id=1, source_target_pairs={{1,0},{12,13},{18,19},{31,30},{33,32},{44,45},{50,51},{63,62},{65,... | collective-permute-start | bytes 7077896 | tf_op jit(solution)/shard_map/ppermute | solution.py:128
  60.2 32.6 %collective-permute-start.18 = (bf16[24,128,128]{2,1,0:T(8,128)(2,1)S(1)}, bf16[24,128,128]{2,1,0:T(8,128)(2,1)S(1)}, u32[]{:S(2)}, u32[]{:S(2)}) collective-permute-start(bf16[24,128,128]{2,1,0:T(8,128)(2,1)S(1)} %collective-permute-done.17.refs_14_), channel_id=1, source_target_pairs={{0,16},{2,18},{4,20},{5,21},{8,24},{9,25},{13,29},{15,31},{17,1},{... | collective-permute-start | bytes 2359304 | tf_op jit(solution)/shard_map/ppermute | solution.py:128
  62.4 45.6 %collective-permute-start.20 = (bf16[72,128,128]{2,1,0:T(8,128)(2,1)}, bf16[72,128,128]{2,1,0:T(8,128)(2,1)}, u32[]{:S(2)}, u32[]{:S(2)}) collective-permute-start(bf16[72,128,128]{2,1,0:T(8,128)(2,1)} %collective-permute-done.10.refs_18_), channel_id=1, source_target_pairs={{1,17},{12,28},{18,2},{31,15},{33,49},{44,60},{50,34},{63,47},{65,... | collective-permute-start | bytes 7077896 | tf_op jit(solution)/shard_map/ppermute | solution.py:128
  70.4 56.7 %collective-permute-start.21 = (bf16[96,128,128]{2,1,0:T(8,128)(2,1)}, bf16[96,128,128]{2,1,0:T(8,128)(2,1)}, u32[]{:S(2)}, u32[]{:S(2)}) collective-permute-start(bf16[96,128,128]{2,1,0:T(8,128)(2,1)} %collective-permute-done.4.refs_2_), channel_id=1, source_target_pairs={{2,3},{3,2},{6,7},{7,6},{10,11},{11,10},{14,15},{15,14},{16,17},{1... | collective-permute-start | bytes 9437192 | tf_op jit(solution)/shard_map/ppermute | solution.py:128
  91.5 16.8 %collective-permute-start.1 = (bf16[72,128,128]{2,1,0:T(8,128)(2,1)}, bf16[72,128,128]{2,1,0:T(8,128)(2,1)}, u32[]{:S(2)}, u32[]{:S(2)}) collective-permute-start(bf16[72,128,128]{2,1,0:T(8,128)(2,1)} %collective-permute-done.refs_0_), channel_id=1, source_target_pairs={{0,16},{1,17},{4,20},{5,21},{8,24},{9,25},{12,28},{13,29},{18,2},{... | collective-permute-start | bytes 7077896 | tf_op jit(solution)/shard_map/ppermute | solution.py:128
  93.7 29.9 %collective-permute-start.7 = (bf16[72,128,128]{2,1,0:T(8,128)(2,1)}, bf16[72,128,128]{2,1,0:T(8,128)(2,1)}, u32[]{:S(2)}, u32[]{:S(2)}) collective-permute-start(bf16[72,128,128]{2,1,0:T(8,128)(2,1)} %constant_dynamic-slice_fusion.5), channel_id=1, source_target_pairs={{2,6},{6,10},{7,3},{10,14},{11,7},{15,11},{17,21},{20,16},{21,25},... | collective-permute-start | bytes 7077896 | tf_op jit(solution)/shard_map/ppermute | solution.py:128
  95.0 37.4 %collective-permute-start.3 = (bf16[72,128,128]{2,1,0:T(8,128)(2,1)}, bf16[72,128,128]{2,1,0:T(8,128)(2,1)}, u32[]{:S(2)}, u32[]{:S(2)}) collective-permute-start(bf16[72,128,128]{2,1,0:T(8,128)(2,1)} %collective-permute-done.2.refs_2_), channel_id=1, source_target_pairs={{3,19},{14,30},{16,0},{29,13},{35,51},{46,62},{48,32},{61,45},{67,... | collective-permute-start | bytes 7077896 | tf_op jit(solution)/shard_map/ppermute | solution.py:128
  108.0 54.7 %collective-permute-start.25 = (bf16[96,128,128]{2,1,0:T(8,128)(2,1)}, bf16[96,128,128]{2,1,0:T(8,128)(2,1)}, u32[]{:S(2)}, u32[]{:S(2)}) collective-permute-start(bf16[96,128,128]{2,1,0:T(8,128)(2,1)} %collective-permute-done.4.refs_2_), channel_id=1, source_target_pairs={{0,16},{1,17},{2,18},{3,19},{4,20},{5,21},{6,22},{7,23},{8,24},{9,... | collective-permute-start | bytes 9437192 | tf_op jit(solution)/shard_map/ppermute | solution.py:128
  108.2 53.2 %collective-permute-start.5 = (bf16[72,128,128]{2,1,0:T(8,128)(2,1)}, bf16[72,128,128]{2,1,0:T(8,128)(2,1)}, u32[]{:S(2)}, u32[]{:S(2)}) collective-permute-start(bf16[72,128,128]{2,1,0:T(8,128)(2,1)} %constant_dynamic-slice_fusion.4), channel_id=1, source_target_pairs={{0,4},{1,110},{3,7},{4,8},{5,1},{6,2},{7,11},{8,12},{9,5},{10,6},{... | collective-permute-start | bytes 7077896 | tf_op jit(solution)/shard_map/ppermute | solution.py:128
  123.5 47.7 %collective-permute-start.8 = (bf16[72,128,128]{2,1,0:T(8,128)(2,1)}, bf16[72,128,128]{2,1,0:T(8,128)(2,1)}, u32[]{:S(2)}, u32[]{:S(2)}) collective-permute-start(bf16[72,128,128]{2,1,0:T(8,128)(2,1)} %collective-permute-done.7.refs_16_), channel_id=1, source_target_pairs={{3,2},{6,7},{7,6},{10,11},{11,10},{14,15},{16,17},{20,21},{21,20},... | collective-permute-start | bytes 7077896 | tf_op jit(solution)/shard_map/ppermute | solution.py:128
  127.1 47.7 %collective-permute-start.26 = (bf16[96,128,128]{2,1,0:T(8,128)(2,1)}, bf16[96,128,128]{2,1,0:T(8,128)(2,1)}, u32[]{:S(2)}, u32[]{:S(2)}) collective-permute-start(bf16[96,128,128]{2,1,0:T(8,128)(2,1)} %collective-permute-done.21.refs_4_), channel_id=1, source_target_pairs={{2,18},{3,19},{6,22},{7,23},{10,26},{11,27},{14,30},{15,31},{16,0}... | collective-permute-start | bytes 9437192 | tf_op jit(solution)/shard_map/ppermute | solution.py:128
  132.3 36.2 %collective-permute-start.22 = (bf16[24,128,128]{2,1,0:T(8,128)(2,1)}, bf16[24,128,128]{2,1,0:T(8,128)(2,1)}, u32[]{:S(2)}, u32[]{:S(2)}) collective-permute-start(bf16[24,128,128]{2,1,0:T(8,128)(2,1)} %constant_dynamic-slice_fusion), channel_id=1, source_target_pairs={{2,6},{3,12},{6,10},{7,3},{10,14},{11,7},{14,33},{15,11},{16,127},... | collective-permute-start | bytes 2359304 | tf_op jit(solution)/shard_map/ppermute | solution.py:128
  161.5 32.5 %collective-permute-start.12 = (bf16[72,128,128]{2,1,0:T(8,128)(2,1)}, bf16[72,128,128]{2,1,0:T(8,128)(2,1)}, u32[]{:S(2)}, u32[]{:S(2)}) collective-permute-start(bf16[72,128,128]{2,1,0:T(8,128)(2,1)} %collective-permute-done.11.refs_8_), channel_id=1, source_target_pairs={{0,16},{13,29},{19,3},{30,14},{32,48},{45,61},{51,35},{62,46},{64,... | collective-permute-start | bytes 7077896 | tf_op jit(solution)/shard_map/ppermute | solution.py:128
  162.8 31.2 %collective-permute-start.19 = (bf16[72,128,128]{2,1,0:T(8,128)(2,1)}, bf16[72,128,128]{2,1,0:T(8,128)(2,1)}, u32[]{:S(2)}, u32[]{:S(2)}) collective-permute-start(bf16[72,128,128]{2,1,0:T(8,128)(2,1)} %collective-permute-done.7.refs_16_), channel_id=1, source_target_pairs={{3,19},{6,22},{7,23},{10,26},{11,27},{14,30},{16,0},{20,4},{21,5},... | collective-permute-start | bytes 7077896 | tf_op jit(solution)/shard_map/ppermute | solution.py:128
  168.5 25.4 %collective-permute-start.6 = (bf16[72,128,128]{2,1,0:T(8,128)(2,1)}, bf16[72,128,128]{2,1,0:T(8,128)(2,1)}, u32[]{:S(2)}, u32[]{:S(2)}) collective-permute-start(bf16[72,128,128]{2,1,0:T(8,128)(2,1)} %collective-permute-done.5.refs_4_), channel_id=1, source_target_pairs={{1,17},{2,18},{3,19},{4,20},{5,21},{6,22},{7,23},{8,24},{9,25},{10... | collective-permute-start | bytes 7077896 | tf_op jit(solution)/shard_map/ppermute | solution.py:128
  171.3 22.8 %collective-permute-start.9 = (bf16[72,128,128]{2,1,0:T(8,128)(2,1)}, bf16[72,128,128]{2,1,0:T(8,128)(2,1)}, u32[]{:S(2)}, u32[]{:S(2)}) collective-permute-start(bf16[72,128,128]{2,1,0:T(8,128)(2,1)} %collective-permute-done.8.refs_6_), channel_id=1, source_target_pairs={{2,18},{6,22},{7,23},{10,26},{11,27},{15,31},{17,1},{20,4},{21,5},... | collective-permute-start | bytes 7077896 | tf_op jit(solution)/shard_map/ppermute | solution.py:128
  174.9 19.1 %collective-permute-start.23 = (bf16[24,128,128]{2,1,0:T(8,128)(2,1)}, bf16[24,128,128]{2,1,0:T(8,128)(2,1)}, u32[]{:S(2)}, u32[]{:S(2)}) collective-permute-start(bf16[24,128,128]{2,1,0:T(8,128)(2,1)} %collective-permute-done.22.refs_20_), channel_id=1, source_target_pairs={{1,17},{3,19},{6,22},{7,23},{10,26},{11,27},{12,28},{14,30},{16,0}... | collective-permute-start | bytes 2359304 | tf_op jit(solution)/shard_map/ppermute | solution.py:128
  207.9 38.4 %collective-permute-start.27 = (bf16[24,128,128]{2,1,0:T(8,128)(2,1)S(1)}, bf16[24,128,128]{2,1,0:T(8,128)(2,1)S(1)}, u32[]{:S(2)}, u32[]{:S(2)}) collective-permute-start(bf16[24,128,128]{2,1,0:T(8,128)(2,1)S(1)} %get-tuple-element.21), channel_id=1, source_target_pairs={{0,0},{16,1},{1,2},{17,3},{3,16},{19,17},{2,18},{18,19},{4,4},{20,... | collective-permute-start | bytes 2359304 | tf_op jit(solution)/shard_map/ppermute | solution.py:128
  209.8 37.9 %collective-permute-start.28 = (bf16[24,128,128]{2,1,0:T(8,128)(2,1)S(1)}, bf16[24,128,128]{2,1,0:T(8,128)(2,1)S(1)}, u32[]{:S(2)}, u32[]{:S(2)}) collective-permute-start(bf16[24,128,128]{2,1,0:T(8,128)(2,1)S(1)} %get-tuple-element.22), channel_id=1, source_target_pairs={{0,1},{16,0},{1,3},{17,2},{3,17},{19,16},{2,19},{18,18},{4,5},{20,... | collective-permute-start | bytes 2359304 | tf_op jit(solution)/shard_map/ppermute | solution.py:128
  211.7 35.9 %collective-permute-start.29 = (bf16[24,128,128]{2,1,0:T(8,128)(2,1)S(1)}, bf16[24,128,128]{2,1,0:T(8,128)(2,1)S(1)}, u32[]{:S(2)}, u32[]{:S(2)}) collective-permute-start(bf16[24,128,128]{2,1,0:T(8,128)(2,1)S(1)} %get-tuple-element.23), channel_id=1, source_target_pairs={{0,2},{16,3},{1,0},{17,1},{3,18},{19,19},{2,16},{18,17},{4,6},{20,... | collective-permute-start | bytes 2359304 | tf_op jit(solution)/shard_map/ppermute | solution.py:128
  216.6 31.1 %collective-permute-start.30 = (bf16[24,128,128]{2,1,0:T(8,128)(2,1)S(1)}, bf16[24,128,128]{2,1,0:T(8,128)(2,1)S(1)}, u32[]{:S(2)}, u32[]{:S(2)}) collective-permute-start(bf16[24,128,128]{2,1,0:T(8,128)(2,1)S(1)} %get-tuple-element.24), channel_id=1, source_target_pairs={{0,3},{16,2},{1,1},{17,0},{3,19},{19,18},{2,17},{18,16},{4,7},{20,... | collective-permute-start | bytes 2359304 | tf_op jit(solution)/shard_map/ppermute | solution.py:128
  (8 other events, 134.4 us)

commit v3 on v2

--- a/solution.py
+++ b/solution.py
@@ -169,8 +169,9 @@
             @pl.when(count == groups)
             def _():
                 if groups == 0:
-                    put(2 * p, jnp.zeros((4 * B, B), F32))
-                    put(2 * p + 1, jnp.zeros((4 * B, B), F32))
+                    if after is not None:
+                        put(2 * p, jnp.zeros((4 * B, B), F32))
+                        put(2 * p + 1, jnp.zeros((4 * B, B), F32))
                     return
                 lhs = left[:, pl.ds(pl.multiple_of(lead * 4 * B, 4 * B), groups * 4 * B)]
                 rows = []
@@ -247,8 +248,10 @@
 def second_kernel(tab, *refs):
     own_w, own_w2, r_w, relay, relay2 = (refs[2 * q : 2 * q + 2] for q in range(5))
     own_n, own_n2, r_n, r_x, own_x, z_n = (refs[10 + 2 * q : 12 + 2 * q] for q in range(6))
-    left, acc = refs[22:24]
-    outs, raw, total, sems = refs[24:28], *refs[28:]
+    far, acc = refs[22:24]
+    outs, raw, total, left, sems, early = refs[24:28], *refs[28:]
+    sums = pltpu.make_async_copy(acc, total, early.at[0])
+    side_copy = pltpu.make_async_copy(far, left, early.at[1])
     loads = Loads(raw, sems)
     edge = (tab[PLACE] == 0) | (tab[PLACE] == 3)
     inside = jnp.logical_not(edge)
@@ -282,10 +285,14 @@
             288 + (2 + side) * 24, 24, inside,
         )
     raw[ZERO] = jnp.zeros((B, B), BF)
+    side_copy.start()
+    sums.start()
     loads.wait()
+    side_copy.wait()
+    sums.wait()
 
     def put(c, value):
-        total[c] = acc[c] + value
+        total[c] += value
 
     base = 12 - 4 * tab[PLACE]
     origins = [jnp.where(4 * g < base, 4 * g, 4 * g + 16) for g in range(3)]
@@ -451,8 +458,11 @@
     more = [own_w, own_w_s, own_w2, own_w2_s, r_w, r_w_s, relay, relay_s, relay2, relay2_s]
     more += [own_n, own_n_s, own_n2, own_n2_s, r_n, r_n_s, r_x, r_x_s, own_x, own_x_s, z_n, z_n_s]
     ready = call(
-        second_kernel, tab, more, [far, acc], [OUT] * 4,
-        [pltpu.VMEM((ZERO + 1, B, B), BF), pltpu.VMEM((WIN, 4 * B, B), F32), sems(12)],
+        second_kernel, tab, more + [far, acc], [], [OUT] * 4,
+        [
+            pltpu.VMEM((ZERO + 1, B, B), BF), pltpu.VMEM((WIN, 4 * B, B), F32),
+            pltpu.VMEM((4 * B, 12 * B), BF), sems(12), sems(2),
+        ],
         36, 6 * 10**9, 22 * 10**6,
     )
     parts = [send(v, pairs_out(k, range(4))) for k, v in enumerate(ready)]

time: 250 us -> 249 us (level)
  no operation moved by 1% of the time
where the time goes in v3:
time: 249 us
  starting transfers between devices  106 us (43%)
  waiting for transfers between devices  88.9 us (36%)
  Pallas kernels  31.5 us (13%)
  local copies, waits for them, and re-layouts  21 us (8%)
    ppermute x31, starting transfers between devices, send(): return lax.ppermute(value, AXES, pairs)  106 us
    ppermute x31, waiting for transfers between devices, send(): return lax.ppermute(value, AXES, pairs)  88.9 us
    pallas_call x3, Pallas kernels, call(): pl.pallas_call(body, out_shape=outs, grid_spec=pltpu.PrefetchScalarGridSp...  31.5 us
    dynamic_slice x7, local copies, waits for them, and re-layouts, cut(): return lax.dynamic_slice_in_dim(a, at, size, 0)  16.3 us
  transfers between devices with their start and end apart: 31, of which 7 were waited for; matrix products, arithmetic and copies ran while one was open for 8% of the time, Pallas kernels for 7%

profile of v3, /device:TPU:1, one launch (start us, length us, event | category | flops | bytes accessed | tf_op | source)
XLA Modules:
  0.0 248.8 jit_solution(17938230700333975442)
XLA Ops:
  0.0 3.9 %collective-permute-start.4 = (bf16[96,128,128]{2,1,0:T(8,128)(2,1)}, bf16[96,128,128]{2,1,0:T(8,128)(2,1)}, u32[]{:S(2)}, u32[]{:S(2)}) collective-permute-start(bf16[96,128,128]{2,1,0:T(8,128)(2,1)} %bitcast.36), channel_id=1, source_target_pairs={{0,1},{1,0},{2,17},{3,16},{4,5},{5,4},{6,21},{7,20},{8,9},{9,8},{1... | collective-permute-start | bytes 9437192 | tf_op jit(solution)/shard_map/ppermute | solution.py:128
  3.9 3.5 %constant_dynamic-slice_fusion.6 = bf16[72,128,128]{2,1,0:T(8,128)(2,1)} fusion(bf16[96,128,128]{2,1,0:T(8,128)(2,1)} %bitcast.37, s32[]{:T(128)S(6)} %select_n.339), kind=kLoop, calls=%fused_computation.26 | loop fusion | bytes 4718596 | tf_op jit(solution)/shard_map/dynamic_slice | solution.py:411
  12.8 1.7 constant_dynamic-slice_fusion.2
  14.5 13.9 %collective-permute-start.10 = (bf16[72,128,128]{2,1,0:T(8,128)(2,1)}, bf16[72,128,128]{2,1,0:T(8,128)(2,1)}, u32[]{:S(2)}, u32[]{:S(2)}) collective-permute-start(bf16[72,128,128]{2,1,0:T(8,128)(2,1)} %constant_dynamic-slice_fusion.2), channel_id=1, source_target_pairs={{16,12},{29,33},{3,127},{14,18},{48,44},{61,65},{35,31},{46,50},{8... | collective-permute-start | bytes 7077896 | tf_op jit(solution)/shard_map/ppermute | solution.py:128
  29.7 2.1 collective-permute-start
  33.9 13.9 %collective-permute-done.4.refs_2_ = bf16[96,128,128]{2,1,0:T(8,128)(2,1)} collective-permute-done((bf16[96,128,128]{2,1,0:T(8,128)(2,1)}, bf16[96,128,128]{2,1,0:T(8,128)(2,1)}, u32[]{:S(2)}, u32[]{:S(2)}) %collective-permute-start.4) | collective-permute-done | bytes 3145760 | tf_op jit(solution)/shard_map/ppermute | solution.py:128
  49.4 3.4 %constant_dynamic-slice_fusion.5 = bf16[72,128,128]{2,1,0:T(8,128)(2,1)} fusion(bf16[96,128,128]{2,1,0:T(8,128)(2,1)} %collective-permute-done.4.refs_2_, s32[]{:T(128)S(6)} %select_n.340), kind=kLoop, calls=%fused_computation.25 | loop fusion | bytes 4718596 | tf_op jit(solution)/shard_map/dynamic_slice | solution.py:411
  52.8 3.4 %constant_dynamic-slice_fusion.4 = bf16[72,128,128]{2,1,0:T(8,128)(2,1)} fusion(bf16[96,128,128]{2,1,0:T(8,128)(2,1)} %collective-permute-done.4.refs_2_, s32[]{:T(128)S(6)} %select_n.341), kind=kLoop, calls=%fused_computation.24 | loop fusion | bytes 4718596 | tf_op jit(solution)/shard_map/dynamic_slice | solution.py:411
  58.1 2.1 collective-permute-start.11
  62.4 2.0 collective-permute-start.20
  64.4 6.0 %collective-permute-done.2.refs_2_ = bf16[72,128,128]{2,1,0:T(8,128)(2,1)} collective-permute-done((bf16[72,128,128]{2,1,0:T(8,128)(2,1)}, bf16[72,128,128]{2,1,0:T(8,128)(2,1)}, u32[]{:S(2)}, u32[]{:S(2)}) %collective-permute-start.2) | collective-permute-done | bytes 2359328 | tf_op jit(solution)/shard_map/ppermute | solution.py:128
  70.4 21.0 %collective-permute-start.21 = (bf16[96,128,128]{2,1,0:T(8,128)(2,1)}, bf16[96,128,128]{2,1,0:T(8,128)(2,1)}, u32[]{:S(2)}, u32[]{:S(2)}) collective-permute-start(bf16[96,128,128]{2,1,0:T(8,128)(2,1)} %collective-permute-done.4.refs_2_), channel_id=1, source_target_pairs={{2,3},{3,2},{6,7},{7,6},{10,11},{11,10},{14,15},{15,14},{16,17},{1... | collective-permute-start | bytes 9437192 | tf_op jit(solution)/shard_map/ppermute | solution.py:128
  95.0 13.1 %collective-permute-start.3 = (bf16[72,128,128]{2,1,0:T(8,128)(2,1)}, bf16[72,128,128]{2,1,0:T(8,128)(2,1)}, u32[]{:S(2)}, u32[]{:S(2)}) collective-permute-start(bf16[72,128,128]{2,1,0:T(8,128)(2,1)} %collective-permute-done.2.refs_2_), channel_id=1, source_target_pairs={{3,19},{14,30},{16,0},{29,13},{35,51},{46,62},{48,32},{61,45},{67,... | collective-permute-start | bytes 7077896 | tf_op jit(solution)/shard_map/ppermute | solution.py:128
  108.2 1.9 collective-permute-start.5
  110.2 13.4 %collective-permute-done.7.refs_16_ = bf16[72,128,128]{2,1,0:T(8,128)(2,1)} collective-permute-done((bf16[72,128,128]{2,1,0:T(8,128)(2,1)}, bf16[72,128,128]{2,1,0:T(8,128)(2,1)}, u32[]{:S(2)}, u32[]{:S(2)}) %collective-permute-start.7) | collective-permute-done | bytes 2359328 | tf_op jit(solution)/shard_map/ppermute | solution.py:128
  123.5 2.8 %collective-permute-start.8 = (bf16[72,128,128]{2,1,0:T(8,128)(2,1)}, bf16[72,128,128]{2,1,0:T(8,128)(2,1)}, u32[]{:S(2)}, u32[]{:S(2)}) collective-permute-start(bf16[72,128,128]{2,1,0:T(8,128)(2,1)} %collective-permute-done.7.refs_16_), channel_id=1, source_target_pairs={{3,2},{6,7},{7,6},{10,11},{11,10},{14,15},{16,17},{20,21},{21,20},... | collective-permute-start | bytes 7077896 | tf_op jit(solution)/shard_map/ppermute | solution.py:128
  127.1 3.0 %collective-permute-start.26 = (bf16[96,128,128]{2,1,0:T(8,128)(2,1)}, bf16[96,128,128]{2,1,0:T(8,128)(2,1)}, u32[]{:S(2)}, u32[]{:S(2)}) collective-permute-start(bf16[96,128,128]{2,1,0:T(8,128)(2,1)} %collective-permute-done.21.refs_4_), channel_id=1, source_target_pairs={{2,18},{3,19},{6,22},{7,23},{10,26},{11,27},{14,30},{15,31},{16,0}... | collective-permute-start | bytes 9437192 | tf_op jit(solution)/shard_map/ppermute | solution.py:128
  130.2 2.1 constant_dynamic-slice_fusion
  132.3 1.9 collective-permute-start.22
  135.3 26.1 %collective-permute-done.5.refs_4_ = bf16[72,128,128]{2,1,0:T(8,128)(2,1)} collective-permute-done((bf16[72,128,128]{2,1,0:T(8,128)(2,1)}, bf16[72,128,128]{2,1,0:T(8,128)(2,1)}, u32[]{:S(2)}, u32[]{:S(2)}) %collective-permute-start.5) | collective-permute-done | bytes 2359328 | tf_op jit(solution)/shard_map/ppermute | solution.py:128
  162.8 5.8 %collective-permute-start.19 = (bf16[72,128,128]{2,1,0:T(8,128)(2,1)}, bf16[72,128,128]{2,1,0:T(8,128)(2,1)}, u32[]{:S(2)}, u32[]{:S(2)}) collective-permute-start(bf16[72,128,128]{2,1,0:T(8,128)(2,1)} %collective-permute-done.7.refs_16_), channel_id=1, source_target_pairs={{3,19},{6,22},{7,23},{10,26},{11,27},{14,30},{16,0},{20,4},{21,5},... | collective-permute-start | bytes 7077896 | tf_op jit(solution)/shard_map/ppermute | solution.py:128
  168.5 2.7 %collective-permute-start.6 = (bf16[72,128,128]{2,1,0:T(8,128)(2,1)}, bf16[72,128,128]{2,1,0:T(8,128)(2,1)}, u32[]{:S(2)}, u32[]{:S(2)}) collective-permute-start(bf16[72,128,128]{2,1,0:T(8,128)(2,1)} %collective-permute-done.5.refs_4_), channel_id=1, source_target_pairs={{1,17},{2,18},{3,19},{4,20},{5,21},{6,22},{7,23},{8,24},{9,25},{10... | collective-permute-start | bytes 7077896 | tf_op jit(solution)/shard_map/ppermute | solution.py:128
  171.3 2.0 collective-permute-start.9
  174.9 2.2 collective-permute-start.23
  177.4 16.6 %shard_map.37 = (f32[28,512,128]{2,1,0:T(8,128)}, bf16[512,1536]{1,0:T(8,128)(2,1)S(1)}) custom-call(s32[999]{0:T(1024)S(1)} %concatenate.53.tab, bf16[96,128,128]{2,1,0:T(8,128)(2,1)S(1)} %bitcast.41, bf16[96,128,128]{2,1,0:T(8,128)(2,1)} %collective-permute-done.24.refs_1_, bf16[96,128,128]{2,1,0:T(8,128)(2,1)} %collective-permute-done.4.refs_2_, ...), custom_call_target="tpu_custom_call" | custom-call | flops 8000000000 | bytes 22000000 | tf_op jit(solution)/shard_map/pallas_call | solution.py:326
  194.1 12.9 %shard_map.38 = (bf16[24,128,128]{2,1,0:T(8,128)(2,1)S(1)}, bf16[24,128,128]{2,1,0:T(8,128)(2,1)S(1)}, bf16[24,128,128]{2,1,0:T(8,128)(2,1)S(1)}, bf16[24,128,128]{2,1,0:T(8,128)(2,1)S(1)}) custom-call(s32[999]{0:T(1024)S(1)} %concatenate.53.tab, bf16[72,128,128]{2,1,0:T(8,128)(2,1)} %collective-permute-done.refs_0_, ...), custom_call_target="tpu_custom_call" | custom-call | flops 6000000000 | bytes 22000000 | tf_op jit(solution)/shard_map/pallas_call | solution.py:326
  207.0 1.9 collective-permute-start.27
  208.9 1.9 collective-permute-start.28
  210.8 4.9 %collective-permute-start.29 = (bf16[24,128,128]{2,1,0:T(8,128)(2,1)S(1)}, bf16[24,128,128]{2,1,0:T(8,128)(2,1)S(1)}, u32[]{:S(2)}, u32[]{:S(2)}) collective-permute-start(bf16[24,128,128]{2,1,0:T(8,128)(2,1)S(1)} %get-tuple-element.23), channel_id=1, source_target_pairs={{0,2},{16,3},{1,0},{17,1},{3,18},{19,19},{2,16},{18,17},{4,6},{20,... | collective-permute-start | bytes 2359304 | tf_op jit(solution)/shard_map/ppermute | solution.py:128
  215.7 2.2 collective-permute-start.30
  217.9 27.5 %collective-permute-done.27.refs_0_ = bf16[24,128,128]{2,1,0:T(8,128)(2,1)S(1)} collective-permute-done((bf16[24,128,128]{2,1,0:T(8,128)(2,1)S(1)}, bf16[24,128,128]{2,1,0:T(8,128)(2,1)S(1)}, u32[]{:S(2)}, u32[]{:S(2)}) %collective-permute-start.27) | collective-permute-done | bytes 786464 | tf_op jit(solution)/shard_map/ppermute | solution.py:128
  246.8 2.0 shard_map.39
  (102 shorter events, 24.6 us)
Async XLA Ops:
  0.0 47.8 %collective-permute-start.4 = (bf16[96,128,128]{2,1,0:T(8,128)(2,1)}, bf16[96,128,128]{2,1,0:T(8,128)(2,1)}, u32[]{:S(2)}, u32[]{:S(2)}) collective-permute-start(bf16[96,128,128]{2,1,0:T(8,128)(2,1)} %bitcast.36), channel_id=1, source_target_pairs={{0,1},{1,0},{2,17},{3,16},{4,5},{5,4},{6,21},{7,20},{8,9},{9,8},{1... | collective-permute-start | bytes 9437192 | tf_op jit(solution)/shard_map/ppermute | solution.py:128
  8.4 3.1 %collective-permute-start.13 = (bf16[24,128,128]{2,1,0:T(8,128)(2,1)}, bf16[24,128,128]{2,1,0:T(8,128)(2,1)}, u32[]{:S(2)}, u32[]{:S(2)}) collective-permute-start(bf16[24,128,128]{2,1,0:T(8,128)(2,1)} %constant_dynamic-slice_fusion.3), channel_id=1, source_target_pairs={{1,5},{4,0},{5,9},{8,4},{9,13},{12,8},{18,22},{22,26},{23,19},{26,... | collective-permute-start | bytes 2359304 | tf_op jit(solution)/shard_map/ppermute | solution.py:128
  10.0 19.7 %collective-permute-start.15 = (bf16[24,128,128]{2,1,0:T(8,128)(2,1)}, bf16[24,128,128]{2,1,0:T(8,128)(2,1)}, u32[]{:S(2)}, u32[]{:S(2)}) collective-permute-start(bf16[24,128,128]{2,1,0:T(8,128)(2,1)} %constant_dynamic-slice_fusion.3), channel_id=1, source_target_pairs={{0,111},{13,2},{19,28},{30,49},{32,15},{45,34},{51,60},{62,81},{64... | collective-permute-start | bytes 2359304 | tf_op jit(solution)/shard_map/ppermute | solution.py:128
  11.5 20.3 %collective-permute-start.14 = (bf16[24,128,128]{2,1,0:T(8,128)(2,1)}, bf16[24,128,128]{2,1,0:T(8,128)(2,1)S(1)}, u32[]{:S(2)}, u32[]{:S(2)}) collective-permute-start(bf16[24,128,128]{2,1,0:T(8,128)(2,1)} %collective-permute-done.13.refs_10_), channel_id=1, source_target_pairs={{0,16},{4,20},{5,21},{8,24},{9,25},{13,29},{19,3},{22,6},{23,7},{2... | collective-permute-start | bytes 2359304 | tf_op jit(solution)/shard_map/ppermute | solution.py:128
  14.5 43.6 %collective-permute-start.10 = (bf16[72,128,128]{2,1,0:T(8,128)(2,1)}, bf16[72,128,128]{2,1,0:T(8,128)(2,1)}, u32[]{:S(2)}, u32[]{:S(2)}) collective-permute-start(bf16[72,128,128]{2,1,0:T(8,128)(2,1)} %constant_dynamic-slice_fusion.2), channel_id=1, source_target_pairs={{16,12},{29,33},{3,127},{14,18},{48,44},{61,65},{35,31},{46,50},{8... | collective-permute-start | bytes 7077896 | tf_op jit(solution)/shard_map/ppermute | solution.py:128
  28.4 63.1 %collective-permute-start.24 = (bf16[96,128,128]{2,1,0:T(8,128)(2,1)S(1)}, bf16[96,128,128]{2,1,0:T(8,128)(2,1)}, u32[]{:S(2)}, u32[]{:S(2)}) collective-permute-start(bf16[96,128,128]{2,1,0:T(8,128)(2,1)S(1)} %bitcast.40), channel_id=1, source_target_pairs={{0,16},{1,17},{4,20},{5,21},{8,24},{9,25},{12,28},{13,29},{18,2},{... | collective-permute-start | bytes 9437192 | tf_op jit(solution)/shard_map/ppermute | solution.py:128
  29.7 32.7 %collective-permute-start = (bf16[72,128,128]{2,1,0:T(8,128)(2,1)}, bf16[72,128,128]{2,1,0:T(8,128)(2,1)}, u32[]{:S(2)}, u32[]{:S(2)}) collective-permute-start(bf16[72,128,128]{2,1,0:T(8,128)(2,1)} %constant_dynamic-slice_fusion.6), channel_id=1, source_target_pairs={{0,4},{4,8},{5,1},{8,12},{9,5},{13,9},{19,23},{22,18},{23,27},{26,... | collective-permute-start | bytes 7077896 | tf_op jit(solution)/shard_map/ppermute | solution.py:128
  32.6 37.8 %collective-permute-start.2 = (bf16[72,128,128]{2,1,0:T(8,128)(2,1)}, bf16[72,128,128]{2,1,0:T(8,128)(2,1)}, u32[]{:S(2)}, u32[]{:S(2)}) collective-permute-start(bf16[72,128,128]{2,1,0:T(8,128)(2,1)} %constant_dynamic-slice_fusion.6), channel_id=1, source_target_pairs={{1,110},{12,3},{18,29},{31,48},{33,14},{44,35},{50,61},{63,80},{65... | collective-permute-start | bytes 7077896 | tf_op jit(solution)/shard_map/ppermute | solution.py:128
  47.8 9.6 %collective-permute-start.16 = (bf16[24,128,128]{2,1,0:T(8,128)(2,1)}, bf16[24,128,128]{2,1,0:T(8,128)(2,1)}, u32[]{:S(2)}, u32[]{:S(2)}) collective-permute-start(bf16[24,128,128]{2,1,0:T(8,128)(2,1)} %collective-permute-done.15.refs_12_), channel_id=1, source_target_pairs={{2,18},{15,31},{17,1},{28,12},{34,50},{47,63},{49,33},{60,44},{66,... | collective-permute-start | bytes 2359304 | tf_op jit(solution)/shard_map/ppermute | solution.py:128
  56.2 117.3 %copy-start.8 = (s32[512,24]{0,1:T(8,128)S(1)}, s32[512,24]{0,1:T(8,128)}, u32[]{:S(2)}) copy-start(s32[512,24]{0,1:T(8,128)} %param.4) | copy-start | bytes 147460
  57.4 2.8 %collective-permute-start.17 = (bf16[24,128,128]{2,1,0:T(8,128)(2,1)S(1)}, bf16[24,128,128]{2,1,0:T(8,128)(2,1)S(1)}, u32[]{:S(2)}, u32[]{:S(2)}) collective-permute-start(bf16[24,128,128]{2,1,0:T(8,128)(2,1)S(1)} %constant_dynamic-slice_fusion.1), channel_id=1, source_target_pairs={{0,111},{1,5},{4,0},{5,9},{8,4},{9,13},{12,8},{13,2},{18,22},{19,2... | collective-permute-start | bytes 2359304 | tf_op jit(solution)/shard_map/ppermute | solution.py:128
  58.1 36.8 %collective-permute-start.11 = (bf16[72,128,128]{2,1,0:T(8,128)(2,1)}, bf16[72,128,128]{2,1,0:T(8,128)(2,1)}, u32[]{:S(2)}, u32[]{:S(2)}) collective-permute-start(bf16[72,128,128]{2,1,0:T(8,128)(2,1)} %collective-permute-done.10.refs_18_), channel_id=1, source_target_pairs={{1,0},{12,13},{18,19},{31,30},{33,32},{44,45},{50,51},{63,62},{65,... | collective-permute-start | bytes 7077896 | tf_op jit(solution)/shard_map/ppermute | solution.py:128
  60.2 32.6 %collective-permute-start.18 = (bf16[24,128,128]{2,1,0:T(8,128)(2,1)S(1)}, bf16[24,128,128]{2,1,0:T(8,128)(2,1)S(1)}, u32[]{:S(2)}, u32[]{:S(2)}) collective-permute-start(bf16[24,128,128]{2,1,0:T(8,128)(2,1)S(1)} %collective-permute-done.17.refs_14_), channel_id=1, source_target_pairs={{0,16},{2,18},{4,20},{5,21},{8,24},{9,25},{13,29},{15,31},{17,1},{... | collective-permute-start | bytes 2359304 | tf_op jit(solution)/shard_map/ppermute | solution.py:128
  62.4 45.6 %collective-permute-start.20 = (bf16[72,128,128]{2,1,0:T(8,128)(2,1)}, bf16[72,128,128]{2,1,0:T(8,128)(2,1)}, u32[]{:S(2)}, u32[]{:S(2)}) collective-permute-start(bf16[72,128,128]{2,1,0:T(8,128)(2,1)} %collective-permute-done.10.refs_18_), channel_id=1, source_target_pairs={{1,17},{12,28},{18,2},{31,15},{33,49},{44,60},{50,34},{63,47},{65,... | collective-permute-start | bytes 7077896 | tf_op jit(solution)/shard_map/ppermute | solution.py:128
  70.4 56.7 %collective-permute-start.21 = (bf16[96,128,128]{2,1,0:T(8,128)(2,1)}, bf16[96,128,128]{2,1,0:T(8,128)(2,1)}, u32[]{:S(2)}, u32[]{:S(2)}) collective-permute-start(bf16[96,128,128]{2,1,0:T(8,128)(2,1)} %collective-permute-done.4.refs_2_), channel_id=1, source_target_pairs={{2,3},{3,2},{6,7},{7,6},{10,11},{11,10},{14,15},{15,14},{16,17},{1... | collective-permute-start | bytes 9437192 | tf_op jit(solution)/shard_map/ppermute | solution.py:128
  91.5 16.8 %collective-permute-start.1 = (bf16[72,128,128]{2,1,0:T(8,128)(2,1)}, bf16[72,128,128]{2,1,0:T(8,128)(2,1)}, u32[]{:S(2)}, u32[]{:S(2)}) collective-permute-start(bf16[72,128,128]{2,1,0:T(8,128)(2,1)} %collective-permute-done.refs_0_), channel_id=1, source_target_pairs={{0,16},{1,17},{4,20},{5,21},{8,24},{9,25},{12,28},{13,29},{18,2},{... | collective-permute-start | bytes 7077896 | tf_op jit(solution)/shard_map/ppermute | solution.py:128
  93.7 29.9 %collective-permute-start.7 = (bf16[72,128,128]{2,1,0:T(8,128)(2,1)}, bf16[72,128,128]{2,1,0:T(8,128)(2,1)}, u32[]{:S(2)}, u32[]{:S(2)}) collective-permute-start(bf16[72,128,128]{2,1,0:T(8,128)(2,1)} %constant_dynamic-slice_fusion.5), channel_id=1, source_target_pairs={{2,6},{6,10},{7,3},{10,14},{11,7},{15,11},{17,21},{20,16},{21,25},... | collective-permute-start | bytes 7077896 | tf_op jit(solution)/shard_map/ppermute | solution.py:128
  95.0 37.4 %collective-permute-start.3 = (bf16[72,128,128]{2,1,0:T(8,128)(2,1)}, bf16[72,128,128]{2,1,0:T(8,128)(2,1)}, u32[]{:S(2)}, u32[]{:S(2)}) collective-permute-start(bf16[72,128,128]{2,1,0:T(8,128)(2,1)} %collective-permute-done.2.refs_2_), channel_id=1, source_target_pairs={{3,19},{14,30},{16,0},{29,13},{35,51},{46,62},{48,32},{61,45},{67,... | collective-permute-start | bytes 7077896 | tf_op jit(solution)/shard_map/ppermute | solution.py:128
  108.0 54.7 %collective-permute-start.25 = (bf16[96,128,128]{2,1,0:T(8,128)(2,1)}, bf16[96,128,128]{2,1,0:T(8,128)(2,1)}, u32[]{:S(2)}, u32[]{:S(2)}) collective-permute-start(bf16[96,128,128]{2,1,0:T(8,128)(2,1)} %collective-permute-done.4.refs_2_), channel_id=1, source_target_pairs={{0,16},{1,17},{2,18},{3,19},{4,20},{5,21},{6,22},{7,23},{8,24},{9,... | collective-permute-start | bytes 9437192 | tf_op jit(solution)/shard_map/ppermute | solution.py:128
  108.2 53.2 %collective-permute-start.5 = (bf16[72,128,128]{2,1,0:T(8,128)(2,1)}, bf16[72,128,128]{2,1,0:T(8,128)(2,1)}, u32[]{:S(2)}, u32[]{:S(2)}) collective-permute-start(bf16[72,128,128]{2,1,0:T(8,128)(2,1)} %constant_dynamic-slice_fusion.4), channel_id=1, source_target_pairs={{0,4},{1,110},{3,7},{4,8},{5,1},{6,2},{7,11},{8,12},{9,5},{10,6},{... | collective-permute-start | bytes 7077896 | tf_op jit(solution)/shard_map/ppermute | solution.py:128
  123.5 47.7 %collective-permute-start.8 = (bf16[72,128,128]{2,1,0:T(8,128)(2,1)}, bf16[72,128,128]{2,1,0:T(8,128)(2,1)}, u32[]{:S(2)}, u32[]{:S(2)}) collective-permute-start(bf16[72,128,128]{2,1,0:T(8,128)(2,1)} %collective-permute-done.7.refs_16_), channel_id=1, source_target_pairs={{3,2},{6,7},{7,6},{10,11},{11,10},{14,15},{16,17},{20,21},{21,20},... | collective-permute-start | bytes 7077896 | tf_op jit(solution)/shard_map/ppermute | solution.py:128
  127.1 47.7 %collective-permute-start.26 = (bf16[96,128,128]{2,1,0:T(8,128)(2,1)}, bf16[96,128,128]{2,1,0:T(8,128)(2,1)}, u32[]{:S(2)}, u32[]{:S(2)}) collective-permute-start(bf16[96,128,128]{2,1,0:T(8,128)(2,1)} %collective-permute-done.21.refs_4_), channel_id=1, source_target_pairs={{2,18},{3,19},{6,22},{7,23},{10,26},{11,27},{14,30},{15,31},{16,0}... | collective-permute-start | bytes 9437192 | tf_op jit(solution)/shard_map/ppermute | solution.py:128
  132.3 36.2 %collective-permute-start.22 = (bf16[24,128,128]{2,1,0:T(8,128)(2,1)}, bf16[24,128,128]{2,1,0:T(8,128)(2,1)}, u32[]{:S(2)}, u32[]{:S(2)}) collective-permute-start(bf16[24,128,128]{2,1,0:T(8,128)(2,1)} %constant_dynamic-slice_fusion), channel_id=1, source_target_pairs={{2,6},{3,12},{6,10},{7,3},{10,14},{11,7},{14,33},{15,11},{16,127},... | collective-permute-start | bytes 2359304 | tf_op jit(solution)/shard_map/ppermute | solution.py:128
  161.5 32.5 %collective-permute-start.12 = (bf16[72,128,128]{2,1,0:T(8,128)(2,1)}, bf16[72,128,128]{2,1,0:T(8,128)(2,1)}, u32[]{:S(2)}, u32[]{:S(2)}) collective-permute-start(bf16[72,128,128]{2,1,0:T(8,128)(2,1)} %collective-permute-done.11.refs_8_), channel_id=1, source_target_pairs={{0,16},{13,29},{19,3},{30,14},{32,48},{45,61},{51,35},{62,46},{64,... | collective-permute-start | bytes 7077896 | tf_op jit(solution)/shard_map/ppermute | solution.py:128
  162.8 31.2 %collective-permute-start.19 = (bf16[72,128,128]{2,1,0:T(8,128)(2,1)}, bf16[72,128,128]{2,1,0:T(8,128)(2,1)}, u32[]{:S(2)}, u32[]{:S(2)}) collective-permute-start(bf16[72,128,128]{2,1,0:T(8,128)(2,1)} %collective-permute-done.7.refs_16_), channel_id=1, source_target_pairs={{3,19},{6,22},{7,23},{10,26},{11,27},{14,30},{16,0},{20,4},{21,5},... | collective-permute-start | bytes 7077896 | tf_op jit(solution)/shard_map/ppermute | solution.py:128
  168.5 25.4 %collective-permute-start.6 = (bf16[72,128,128]{2,1,0:T(8,128)(2,1)}, bf16[72,128,128]{2,1,0:T(8,128)(2,1)}, u32[]{:S(2)}, u32[]{:S(2)}) collective-permute-start(bf16[72,128,128]{2,1,0:T(8,128)(2,1)} %collective-permute-done.5.refs_4_), channel_id=1, source_target_pairs={{1,17},{2,18},{3,19},{4,20},{5,21},{6,22},{7,23},{8,24},{9,25},{10... | collective-permute-start | bytes 7077896 | tf_op jit(solution)/shard_map/ppermute | solution.py:128
  171.3 22.8 %collective-permute-start.9 = (bf16[72,128,128]{2,1,0:T(8,128)(2,1)}, bf16[72,128,128]{2,1,0:T(8,128)(2,1)}, u32[]{:S(2)}, u32[]{:S(2)}) collective-permute-start(bf16[72,128,128]{2,1,0:T(8,128)(2,1)} %collective-permute-done.8.refs_6_), channel_id=1, source_target_pairs={{2,18},{6,22},{7,23},{10,26},{11,27},{15,31},{17,1},{20,4},{21,5},... | collective-permute-start | bytes 7077896 | tf_op jit(solution)/shard_map/ppermute | solution.py:128
  174.9 19.1 %collective-permute-start.23 = (bf16[24,128,128]{2,1,0:T(8,128)(2,1)}, bf16[24,128,128]{2,1,0:T(8,128)(2,1)}, u32[]{:S(2)}, u32[]{:S(2)}) collective-permute-start(bf16[24,128,128]{2,1,0:T(8,128)(2,1)} %collective-permute-done.22.refs_20_), channel_id=1, source_target_pairs={{1,17},{3,19},{6,22},{7,23},{10,26},{11,27},{12,28},{14,30},{16,0}... | collective-permute-start | bytes 2359304 | tf_op jit(solution)/shard_map/ppermute | solution.py:128
  207.0 38.4 %collective-permute-start.27 = (bf16[24,128,128]{2,1,0:T(8,128)(2,1)S(1)}, bf16[24,128,128]{2,1,0:T(8,128)(2,1)S(1)}, u32[]{:S(2)}, u32[]{:S(2)}) collective-permute-start(bf16[24,128,128]{2,1,0:T(8,128)(2,1)S(1)} %get-tuple-element.21), channel_id=1, source_target_pairs={{0,0},{16,1},{1,2},{17,3},{3,16},{19,17},{2,18},{18,19},{4,4},{20,... | collective-permute-start | bytes 2359304 | tf_op jit(solution)/shard_map/ppermute | solution.py:128
  208.9 37.9 %collective-permute-start.28 = (bf16[24,128,128]{2,1,0:T(8,128)(2,1)S(1)}, bf16[24,128,128]{2,1,0:T(8,128)(2,1)S(1)}, u32[]{:S(2)}, u32[]{:S(2)}) collective-permute-start(bf16[24,128,128]{2,1,0:T(8,128)(2,1)S(1)} %get-tuple-element.22), channel_id=1, source_target_pairs={{0,1},{16,0},{1,3},{17,2},{3,17},{19,16},{2,19},{18,18},{4,5},{20,... | collective-permute-start | bytes 2359304 | tf_op jit(solution)/shard_map/ppermute | solution.py:128
  210.8 35.9 %collective-permute-start.29 = (bf16[24,128,128]{2,1,0:T(8,128)(2,1)S(1)}, bf16[24,128,128]{2,1,0:T(8,128)(2,1)S(1)}, u32[]{:S(2)}, u32[]{:S(2)}) collective-permute-start(bf16[24,128,128]{2,1,0:T(8,128)(2,1)S(1)} %get-tuple-element.23), channel_id=1, source_target_pairs={{0,2},{16,3},{1,0},{17,1},{3,18},{19,19},{2,16},{18,17},{4,6},{20,... | collective-permute-start | bytes 2359304 | tf_op jit(solution)/shard_map/ppermute | solution.py:128
  215.7 31.1 %collective-permute-start.30 = (bf16[24,128,128]{2,1,0:T(8,128)(2,1)S(1)}, bf16[24,128,128]{2,1,0:T(8,128)(2,1)S(1)}, u32[]{:S(2)}, u32[]{:S(2)}) collective-permute-start(bf16[24,128,128]{2,1,0:T(8,128)(2,1)S(1)} %get-tuple-element.24), channel_id=1, source_target_pairs={{0,3},{16,2},{1,1},{17,0},{3,19},{19,18},{2,17},{18,16},{4,7},{20,... | collective-permute-start | bytes 2359304 | tf_op jit(solution)/shard_map/ppermute | solution.py:128
  (8 other events, 134.4 us)
